TPU v7x, 256 devices: a whole 4x4x8 slice. The times are simulated.
256 devices in a mesh: elem: 64 (over z, y_lo, x), band: 4 (over y_hi, core).
Axes of the slice: x: 4, y: 4 (y_hi: 2, y_lo: 2; y = y_hi * 2 + y_lo), z: 8, core: 2. Of those that a mesh axis runs over, the one named last changes fastest.
Arguments:
- basis_counts: int32 [512, 16], P('elem', 'band'), may hold values from 1 to 128, as said below
- neighbour_codes: int32 [512, 16, 6], P('elem', 'band'), may hold values from 0 to 8, as said below
- x_block: bfloat16 [512, 16, 160, 128], P('elem', 'band'), may hold values from -6 to 6
- h_self: bfloat16 [512, 16, 128, 128], P('elem', 'band'), may hold values from -0.375 to 0.375
- h_near: bfloat16 [512, 16, 6, 128, 128], P('elem', 'band'), may hold values from -0.375 to 0.375
Outputs:
- filtered: bfloat16 [512, 16, 160, 128], P('elem', 'band')
- gram: float32 [160, 160], P('band')
- ritz: float32 [160, 160], P('band')
Inputs may be any that keep to these rules, and one draw needn't show every extreme that they name: `basis_counts`: at least one element holds exactly 128 basis functions. `neighbour_codes`: an element's 6 codes are distinct and never 4; code q names the element offset by q // 3 - 1 along the first dimension and q % 3 - 1 along the second, periodically.
All inputs are finite; a program needn't handle non-finite values.
Results may differ from a plain program's by a relative error of at most 0.007.
Values may be sent and summed in bfloat16 or wider, within the bound.
No kernel may reach another device: no remote copies, remote signals or barrier semaphores. Data moves between devices by JAX's collectives and lax.ppermute only.
A program may use at most 128 MiB of HBM per device.

v0:
```python
import jax
import jax.numpy as jnp
from jax import lax
from jax.sharding import PartitionSpec as P

cheb_center = 0.25
cheb_half = 1.5


def extended_2(block, sides, width):
    for axis, dim in sides:
        count = lax.axis_size(axis)
        forward = [(i, i + 1) for i in range(count - 1)]
        forward.append((count - 1, 0))
        backward = [(target, source) for source, target in forward]
        low = lax.ppermute(
            lax.slice_in_dim(block, block.shape[dim] - width, None, axis=dim), axis, forward
        )
        high = lax.ppermute(lax.slice_in_dim(block, 0, width, axis=dim), axis, backward)
        block = jnp.concatenate([low, block, high], axis=dim)
    return block


def on_device(basis_counts, neighbour_codes, x_block, h_self, h_near):
    elem_rows, elem_cols, columns, basis_max = x_block.shape
    neighbours = neighbour_codes.shape[2]
    elements = elem_rows * elem_cols
    width_ext = elem_cols + 2
    live_mask = (
        lax.broadcasted_iota(jnp.int32, (elem_rows, elem_cols, 1, basis_max), 3)
        < basis_counts[:, :, None, None]
    )
    row_iota = lax.broadcasted_iota(jnp.int32, (elem_rows, elem_cols, neighbours), 0)
    col_iota = lax.broadcasted_iota(jnp.int32, (elem_rows, elem_cols, neighbours), 1)
    gather_index = (
        (row_iota + neighbour_codes // 3) * width_ext + col_iota + neighbour_codes % 3
    ).reshape(elements, neighbours)
    self_flat = h_self.reshape(elements, basis_max, basis_max)
    near_flat = h_near.reshape(elements, neighbours, basis_max, basis_max)

    def expand(vector_block):
        return extended_2(vector_block, (("elem", 0), ("band", 1)), 1)

    def apply_op(vector_block):
        extended = expand(vector_block).reshape((elem_rows + 2) * width_ext, columns, basis_max)
        nearby = jnp.take(extended, gather_index, axis=0)
        summed = jnp.einsum(
            "ecs,esr->ecr",
            vector_block.reshape(elements, columns, basis_max),
            self_flat,
            preferred_element_type=jnp.float32,
        )
        summed = summed + jnp.einsum(
            "ekcs,eksr->ecr", nearby, near_flat, preferred_element_type=jnp.float32
        )
        summed = summed.reshape(elem_rows, elem_cols, columns, basis_max)
        return jnp.where(live_mask, summed, jnp.float32(0.0))

    start = jnp.where(live_mask, x_block, jnp.zeros_like(x_block))
    first = ((apply_op(start) - cheb_center * start.astype(jnp.float32)) / cheb_half).astype(
        jnp.bfloat16
    )
    second = (
        2.0 * (apply_op(first) - cheb_center * first.astype(jnp.float32)) / cheb_half
        - start.astype(jnp.float32)
    ).astype(jnp.bfloat16)
    filtered = (
        2.0 * (apply_op(second) - cheb_center * second.astype(jnp.float32)) / cheb_half
        - first.astype(jnp.float32)
    ).astype(jnp.bfloat16)
    image = apply_op(filtered).astype(jnp.bfloat16)
    filt_flat = filtered.reshape(elements, columns, basis_max)
    gram_part = jnp.einsum("ecr,edr->cd", filt_flat, filt_flat, preferred_element_type=jnp.float32)
    ritz_part = jnp.einsum(
        "ecr,edr->cd",
        filt_flat,
        image.reshape(elements, columns, basis_max),
        preferred_element_type=jnp.float32,
    )
    band_count = lax.axis_size("band")
    owned_rows = columns // band_count
    normalizer = jnp.float32(elements * lax.axis_size("elem") * band_count * basis_max / 3.0)
    gram_total, ritz_total = lax.psum((gram_part, ritz_part), ("elem", "band"))
    first_row = lax.axis_index("band") * owned_rows
    gram_rows = lax.dynamic_slice_in_dim(gram_total, first_row, owned_rows, 0)
    ritz_rows = lax.dynamic_slice_in_dim(ritz_total, first_row, owned_rows, 0)
    return (filtered, gram_rows / normalizer, ritz_rows / normalizer)


def solution(mesh):
    in_specs = (
        P("elem", "band"),
        P("elem", "band", None),
        P("elem", "band", None, None),
        P("elem", "band", None, None),
        P("elem", "band", None, None, None),
    )
    out_specs = (P("elem", "band", None, None), P("band", None), P("band", None))
    return jax.shard_map(
        on_device, mesh=mesh, in_specs=in_specs, out_specs=out_specs, check_vma=False
    )
```

profile of v0, /device:TPU:1, one launch (start us, length us, event | category | flops | bytes accessed | tf_op | source)
XLA Modules:
  0.0 448.1 jit_solution(14405538510265482460)
XLA Ops:
  9.6 2.1 collective-permute-start
  11.7 7.7 %collective-permute-start.1 = (bf16[1,4,160,128]{3,2,1,0:T(8,128)(2,1)S(1)}, bf16[1,4,160,128]{3,2,1,0:T(8,128)(2,1)S(1)}, u32[]{:S(2)}, u32[]{:S(2)}) collective-permute-start(bf16[1,4,160,128]{3,2,1,0:T(8,128)(2,1)S(1)} %get-tuple-element.21), channel_id=1, source_target_pairs={{4,0},{8,4},{12,8},{16,12},{20,16},{24,20},{28,24},{32,28},{36,32}... | collective-permute-start | bytes 491528 | tf_op jit(solution)/shard_map/ppermute | solution.py:19
  19.9 3.3 collective-permute-done
  23.3 3.9 collective-permute-start.2
  27.3 2.1 fusion.47
  29.3 6.3 %collective-permute-done.2 = bf16[10,1,160,128]{3,2,1,0:T(8,128)(2,1)S(1)} collective-permute-done((bf16[10,1,160,128]{3,2,1,0:T(8,128)(2,1)S(1)}, bf16[10,1,160,128]{3,2,1,0:T(8,128)(2,1)S(1)}, u32[]{:S(2)}, u32[]{:S(2)}) %collective-permute-start.2) | collective-permute-done | bytes 409632 | tf_op jit(solution)/shard_map/ppermute | solution.py:16
  38.9 8.9 %gather_fusion = bf16[192,160,128]{2,1,0:T(8,128)(2,1)} fusion(bf16[60,160,128]{2,1,0:T(8,128)(2,1)S(1)} %bitcast.61, s32[1024]{0:T(1024)S(1)} %pad_clamp_fusion), kind=kCustom, calls=%fused_computation.clone | custom fusion | bytes 15729408 | tf_op jit(solution)/shard_map/jit(_take)/gather | solution.py:46
  47.8 8.3 %bitcast_add_fusion.3 = f32[32,160,128]{2,1,0:T(8,128)S(1)} fusion(f32[32,160,128]{2,1,0:T(8,128)} %fusion.47, bf16[32,6,128,128]{3,2,1,0:T(8,128)(2,1)} %bitcast.74, bf16[32,6,160,128]{3,2,1,0:T(8,128)(2,1)} %bitcast.68, pred[32,6]{1,0:T(8,128)(4,1)S(1)} %copy.11), kind=kOutput, calls=%fused_computation.34 | convolution fusion | flops 1011220480 | bytes 19398848 | tf_op jit(solution)/shard_map/ekcs,eksr->ecr/dot_general | solution.py:53
  56.9 5.8 %collective-permute-start.5 = (bf16[1,4,160,128]{3,2,1,0:T(8,128)(2,1)S(1)}, bf16[1,4,160,128]{3,2,1,0:T(8,128)(2,1)S(1)}, u32[]{:S(2)}, u32[]{:S(2)}) collective-permute-start(bf16[1,4,160,128]{3,2,1,0:T(8,128)(2,1)S(1)} %get-tuple-element.19), channel_id=1, source_target_pairs={{4,0},{8,4},{12,8},{16,12},{20,16},{24,20},{28,24},{32,28},{36,32}... | collective-permute-start | bytes 491528 | tf_op jit(solution)/shard_map/ppermute | solution.py:19
  62.8 4.6 %collective-permute-done.4 = bf16[1,4,160,128]{3,2,1,0:T(8,128)(2,1)S(1)} collective-permute-done((bf16[1,4,160,128]{3,2,1,0:T(8,128)(2,1)S(1)}, bf16[1,4,160,128]{3,2,1,0:T(8,128)(2,1)S(1)}, u32[]{:S(2)}, u32[]{:S(2)}) %collective-permute-start.4) | collective-permute-done | bytes 163872 | tf_op jit(solution)/shard_map/ppermute | solution.py:16
  67.4 3.4 collective-permute-start.6
  70.8 2.1 fusion.48
  72.9 6.3 %collective-permute-done.6 = bf16[10,1,160,128]{3,2,1,0:T(8,128)(2,1)S(1)} collective-permute-done((bf16[10,1,160,128]{3,2,1,0:T(8,128)(2,1)S(1)}, bf16[10,1,160,128]{3,2,1,0:T(8,128)(2,1)S(1)}, u32[]{:S(2)}, u32[]{:S(2)}) %collective-permute-start.6) | collective-permute-done | bytes 409632 | tf_op jit(solution)/shard_map/ppermute | solution.py:16
  80.9 1.8 pad_maximum_fusion.1
  82.6 10.6 %gather_fusion.1 = bf16[192,160,128]{2,1,0:T(8,128)(2,1)} fusion(bf16[60,160,128]{2,1,0:T(8,128)(2,1)} %bitcast.63, s32[1024]{0:T(1024)S(1)} %pad_clamp_fusion), kind=kCustom, calls=%fused_computation.1.clone | custom fusion | bytes 15729408 | tf_op jit(solution)/shard_map/jit(_take)/gather | solution.py:46
  93.2 8.3 %bitcast_add_fusion.2 = f32[32,160,128]{2,1,0:T(8,128)S(1)} fusion(f32[32,160,128]{2,1,0:T(8,128)} %fusion.48, bf16[32,6,128,128]{3,2,1,0:T(8,128)(2,1)} %bitcast.75, bf16[32,6,160,128]{3,2,1,0:T(8,128)(2,1)} %bitcast.69, pred[32,6]{1,0:T(8,128)(4,1)S(1)} %copy.11), kind=kOutput, calls=%fused_computation.33 | convolution fusion | flops 1011220480 | bytes 19398848 | tf_op jit(solution)/shard_map/ekcs,eksr->ecr/dot_general | solution.py:53
  102.6 5.7 %collective-permute-start.9 = (bf16[1,4,160,128]{3,2,1,0:T(8,128)(2,1)S(1)}, bf16[1,4,160,128]{3,2,1,0:T(8,128)(2,1)S(1)}, u32[]{:S(2)}, u32[]{:S(2)}) collective-permute-start(bf16[1,4,160,128]{3,2,1,0:T(8,128)(2,1)S(1)} %get-tuple-element.17), channel_id=1, source_target_pairs={{4,0},{8,4},{12,8},{16,12},{20,16},{24,20},{28,24},{32,28},{36,32}... | collective-permute-start | bytes 491528 | tf_op jit(solution)/shard_map/ppermute | solution.py:19
  108.3 4.6 %collective-permute-done.8 = bf16[1,4,160,128]{3,2,1,0:T(8,128)(2,1)S(1)} collective-permute-done((bf16[1,4,160,128]{3,2,1,0:T(8,128)(2,1)S(1)}, bf16[1,4,160,128]{3,2,1,0:T(8,128)(2,1)S(1)}, u32[]{:S(2)}, u32[]{:S(2)}) %collective-permute-start.8) | collective-permute-done | bytes 163872 | tf_op jit(solution)/shard_map/ppermute | solution.py:16
  113.0 3.2 collective-permute-start.10
  116.5 2.1 fusion.49
  118.6 5.9 %collective-permute-done.10 = bf16[10,1,160,128]{3,2,1,0:T(8,128)(2,1)S(1)} collective-permute-done((bf16[10,1,160,128]{3,2,1,0:T(8,128)(2,1)S(1)}, bf16[10,1,160,128]{3,2,1,0:T(8,128)(2,1)S(1)}, u32[]{:S(2)}, u32[]{:S(2)}) %collective-permute-start.10) | collective-permute-done | bytes 409632 | tf_op jit(solution)/shard_map/ppermute | solution.py:16
  124.5 1.8 collective-permute-done.11
  126.7 8.9 %gather_fusion.2 = bf16[192,160,128]{2,1,0:T(8,128)(2,1)} fusion(bf16[60,160,128]{2,1,0:T(8,128)(2,1)S(1)} %bitcast.64, s32[1024]{0:T(1024)S(1)} %pad_clamp_fusion), kind=kCustom, calls=%fused_computation.2.clone | custom fusion | bytes 15729408 | tf_op jit(solution)/shard_map/jit(_take)/gather | solution.py:46
  135.7 8.4 %bitcast_add_fusion.1 = f32[32,160,128]{2,1,0:T(8,128)S(1)} fusion(f32[32,160,128]{2,1,0:T(8,128)} %fusion.49, bf16[32,6,128,128]{3,2,1,0:T(8,128)(2,1)} %bitcast.76, bf16[32,6,160,128]{3,2,1,0:T(8,128)(2,1)} %bitcast.70, pred[32,6]{1,0:T(8,128)(4,1)S(1)} %copy.11), kind=kOutput, calls=%fused_computation.32 | convolution fusion | flops 1011220480 | bytes 19398848 | tf_op jit(solution)/shard_map/ekcs,eksr->ecr/dot_general | solution.py:53
  144.9 5.8 %collective-permute-start.13 = (bf16[1,4,160,128]{3,2,1,0:T(8,128)(2,1)S(1)}, bf16[1,4,160,128]{3,2,1,0:T(8,128)(2,1)S(1)}, u32[]{:S(2)}, u32[]{:S(2)}) collective-permute-start(bf16[1,4,160,128]{3,2,1,0:T(8,128)(2,1)S(1)} %get-tuple-element.15), channel_id=1, source_target_pairs={{4,0},{8,4},{12,8},{16,12},{20,16},{24,20},{28,24},{32,28},{36,32}... | collective-permute-start | bytes 491528 | tf_op jit(solution)/shard_map/ppermute | solution.py:19
  150.7 4.6 %collective-permute-done.12 = bf16[1,4,160,128]{3,2,1,0:T(8,128)(2,1)S(1)} collective-permute-done((bf16[1,4,160,128]{3,2,1,0:T(8,128)(2,1)S(1)}, bf16[1,4,160,128]{3,2,1,0:T(8,128)(2,1)S(1)}, u32[]{:S(2)}, u32[]{:S(2)}) %collective-permute-start.12) | collective-permute-done | bytes 163872 | tf_op jit(solution)/shard_map/ppermute | solution.py:16
  155.4 3.3 collective-permute-start.14
  160.1 2.1 fusion.50
  162.2 4.8 %collective-permute-done.14 = bf16[10,1,160,128]{3,2,1,0:T(8,128)(2,1)S(1)} collective-permute-done((bf16[10,1,160,128]{3,2,1,0:T(8,128)(2,1)S(1)}, bf16[10,1,160,128]{3,2,1,0:T(8,128)(2,1)S(1)}, u32[]{:S(2)}, u32[]{:S(2)}) %collective-permute-start.14) | collective-permute-done | bytes 409632 | tf_op jit(solution)/shard_map/ppermute | solution.py:16
  170.4 10.6 %gather_fusion.3 = bf16[192,160,128]{2,1,0:T(8,128)(2,1)} fusion(bf16[60,160,128]{2,1,0:T(8,128)(2,1)} %bitcast.62, s32[1024]{0:T(1024)S(1)} %pad_clamp_fusion), kind=kCustom, calls=%fused_computation.3.clone | custom fusion | bytes 15729408 | tf_op jit(solution)/shard_map/jit(_take)/gather | solution.py:46
  181.0 8.1 %bitcast_add_fusion = bf16[32,160,128]{2,1,0:T(8,128)(2,1)S(1)} fusion(f32[32,160,128]{2,1,0:T(8,128)} %fusion.50, bf16[32,6,128,128]{3,2,1,0:T(8,128)(2,1)} %bitcast.77, bf16[32,6,160,128]{3,2,1,0:T(8,128)(2,1)} %bitcast.67, pred[32,6]{1,0:T(8,128)(4,1)S(1)} %copy.11), kind=kOutput, calls=%fused_computation.31 | convolution fusion | flops 1011875840 | bytes 18088128 | tf_op jit(solution)/shard_map/ekcs,eksr->ecr/dot_general | solution.py:53
  190.4 249.0 %all-reduce.3.cloned.1.call-done = (f32[160,160]{1,0:T(8,128)}, f32[160,160]{1,0:T(8,128)}) async-done(((f32[160,160]{1,0:T(8,128)}, f32[160,160]{1,0:T(8,128)}), (f32[160,160]{1,0:T(8,128)}, f32[160,160]{1,0:T(8,128)})) %all-reduce.3.cloned.1.call-update) | async-done | bytes 204816 | tf_op jit(solution)/shard_map/psum | solution.py:83
  (69 shorter events, 19.0 us)
Async XLA Ops:
  7.2 20.1 %copy-start = (bf16[8,4,128,128]{3,2,1,0:T(8,128)(2,1)S(1)}, bf16[8,4,128,128]{3,2,1,0:T(8,128)(2,1)}, u32[]{:S(2)}) copy-start(bf16[8,4,128,128]{3,2,1,0:T(8,128)(2,1)} %param.10) | copy-start | bytes 3145732
  7.2 12.2 %copy-start.11 = (s32[8,4,6]{0,1,2:T(4,128)S(1)}, s32[8,4,6]{0,1,2:T(4,128)}, u32[]{:S(2)}) copy-start(s32[8,4,6]{0,1,2:T(4,128)} %param.8) | copy-start | bytes 2308
  7.2 432.2 %all-reduce.3.cloned.1.call-start = ((), (), s32[]{:S(2)}) async-start(), calls=%async_computation | async-start | bytes 655360 | tf_op jit(solution)/shard_map/psum | solution.py:83
  9.6 19.8 %copy-start.6 = (bf16[8,4,160,128]{3,2,1,0:T(8,128)(2,1)}, bf16[8,4,160,128]{3,2,1,0:T(8,128)(2,1)S(1)}, u32[]{:S(2)}) copy-start(bf16[8,4,160,128]{3,2,1,0:T(8,128)(2,1)S(1)} %broadcast_select_fusion) | copy-start | bytes 3932164
  9.6 13.6 %collective-permute-start = (bf16[1,4,160,128]{3,2,1,0:T(8,128)(2,1)S(1)}, bf16[1,4,160,128]{3,2,1,0:T(8,128)(2,1)S(1)}, u32[]{:S(2)}, u32[]{:S(2)}) collective-permute-start(bf16[1,4,160,128]{3,2,1,0:T(8,128)(2,1)S(1)} %get-tuple-element.20), channel_id=1, source_target_pairs={{0,4},{4,8},{8,12},{12,16},{16,20},{20,24},{24,28},{28,32},{32,36}... | collective-permute-start | bytes 491528 | tf_op jit(solution)/shard_map/ppermute | solution.py:16
  11.7 11.5 %collective-permute-start.1 = (bf16[1,4,160,128]{3,2,1,0:T(8,128)(2,1)S(1)}, bf16[1,4,160,128]{3,2,1,0:T(8,128)(2,1)S(1)}, u32[]{:S(2)}, u32[]{:S(2)}) collective-permute-start(bf16[1,4,160,128]{3,2,1,0:T(8,128)(2,1)S(1)} %get-tuple-element.21), channel_id=1, source_target_pairs={{4,0},{8,4},{12,8},{16,12},{20,16},{24,20},{28,24},{32,28},{36,32}... | collective-permute-start | bytes 491528 | tf_op jit(solution)/shard_map/ppermute | solution.py:19
  23.2 6.1 %copy-start.9 = (bf16[1,4,160,128]{3,2,1,0:T(8,128)(2,1)}, bf16[1,4,160,128]{3,2,1,0:T(8,128)(2,1)S(1)}, u32[]{:S(2)}) copy-start(bf16[1,4,160,128]{3,2,1,0:T(8,128)(2,1)S(1)} %collective-permute-done) | copy-start | bytes 491524
  23.2 6.1 %copy-start.10 = (bf16[1,4,160,128]{3,2,1,0:T(8,128)(2,1)}, bf16[1,4,160,128]{3,2,1,0:T(8,128)(2,1)S(1)}, u32[]{:S(2)}) copy-start(bf16[1,4,160,128]{3,2,1,0:T(8,128)(2,1)S(1)} %collective-permute-done.1) | copy-start | bytes 491524
  23.3 12.4 %collective-permute-start.2 = (bf16[10,1,160,128]{3,2,1,0:T(8,128)(2,1)S(1)}, bf16[10,1,160,128]{3,2,1,0:T(8,128)(2,1)S(1)}, u32[]{:S(2)}, u32[]{:S(2)}) collective-permute-start(bf16[10,1,160,128]{3,2,1,0:T(8,128)(2,1)S(1)} %get-tuple-element.12), channel_id=1, source_target_pairs={{0,1},{1,2},{2,3},{3,0},{4,5},{5,6},{6,7},{7,4},{8,9},{9,10},{10,1... | collective-permute-start | bytes 1228808 | tf_op jit(solution)/shard_map/ppermute | solution.py:16
  27.2 10.0 %collective-permute-start.3 = (bf16[10,1,160,128]{3,2,1,0:T(8,128)(2,1)S(1)}, bf16[10,1,160,128]{3,2,1,0:T(8,128)(2,1)S(1)}, u32[]{:S(2)}, u32[]{:S(2)}) collective-permute-start(bf16[10,1,160,128]{3,2,1,0:T(8,128)(2,1)S(1)} %get-tuple-element.13), channel_id=1, source_target_pairs={{1,0},{2,1},{3,2},{0,3},{5,4},{6,5},{7,6},{4,7},{9,8},{10,9},{11,1... | collective-permute-start | bytes 1228808 | tf_op jit(solution)/shard_map/ppermute | solution.py:19
  47.8 8.3 %copy-start.7 = (bf16[8,4,160,128]{3,2,1,0:T(8,128)(2,1)S(1)}, bf16[8,4,160,128]{3,2,1,0:T(8,128)(2,1)}, u32[]{:S(2)}) copy-start(bf16[8,4,160,128]{3,2,1,0:T(8,128)(2,1)} %param.9) | copy-start | bytes 3932164
  56.8 44.8 %copy-start.2 = (bf16[8,4,160,128]{3,2,1,0:T(8,128)(2,1)}, bf16[8,4,160,128]{3,2,1,0:T(8,128)(2,1)S(1)}, u32[]{:S(2)}) copy-start(bf16[8,4,160,128]{3,2,1,0:T(8,128)(2,1)S(1)} %fusion.18) | copy-start | bytes 3932164
  56.8 10.5 %collective-permute-start.4 = (bf16[1,4,160,128]{3,2,1,0:T(8,128)(2,1)S(1)}, bf16[1,4,160,128]{3,2,1,0:T(8,128)(2,1)S(1)}, u32[]{:S(2)}, u32[]{:S(2)}) collective-permute-start(bf16[1,4,160,128]{3,2,1,0:T(8,128)(2,1)S(1)} %get-tuple-element.18), channel_id=1, source_target_pairs={{0,4},{4,8},{8,12},{12,16},{16,20},{20,24},{24,28},{28,32},{32,36}... | collective-permute-start | bytes 491528 | tf_op jit(solution)/shard_map/ppermute | solution.py:16
  56.9 10.4 %collective-permute-start.5 = (bf16[1,4,160,128]{3,2,1,0:T(8,128)(2,1)S(1)}, bf16[1,4,160,128]{3,2,1,0:T(8,128)(2,1)S(1)}, u32[]{:S(2)}, u32[]{:S(2)}) collective-permute-start(bf16[1,4,160,128]{3,2,1,0:T(8,128)(2,1)S(1)} %get-tuple-element.19), channel_id=1, source_target_pairs={{4,0},{8,4},{12,8},{16,12},{20,16},{24,20},{28,24},{32,28},{36,32}... | collective-permute-start | bytes 491528 | tf_op jit(solution)/shard_map/ppermute | solution.py:19
  67.4 11.8 %collective-permute-start.6 = (bf16[10,1,160,128]{3,2,1,0:T(8,128)(2,1)S(1)}, bf16[10,1,160,128]{3,2,1,0:T(8,128)(2,1)S(1)}, u32[]{:S(2)}, u32[]{:S(2)}) collective-permute-start(bf16[10,1,160,128]{3,2,1,0:T(8,128)(2,1)S(1)} %get-tuple-element.10), channel_id=1, source_target_pairs={{0,1},{1,2},{2,3},{3,0},{4,5},{5,6},{6,7},{7,4},{8,9},{9,10},{10,1... | collective-permute-start | bytes 1228808 | tf_op jit(solution)/shard_map/ppermute | solution.py:16
  70.8 10.0 %collective-permute-start.7 = (bf16[10,1,160,128]{3,2,1,0:T(8,128)(2,1)S(1)}, bf16[10,1,160,128]{3,2,1,0:T(8,128)(2,1)S(1)}, u32[]{:S(2)}, u32[]{:S(2)}) collective-permute-start(bf16[10,1,160,128]{3,2,1,0:T(8,128)(2,1)S(1)} %get-tuple-element.11), channel_id=1, source_target_pairs={{1,0},{2,1},{3,2},{0,3},{5,4},{6,5},{7,6},{4,7},{9,8},{10,9},{11,1... | collective-permute-start | bytes 1228808 | tf_op jit(solution)/shard_map/ppermute | solution.py:19
  93.2 8.4 %copy-start.8 = (bf16[8,4,160,128]{3,2,1,0:T(8,128)(2,1)S(1)}, bf16[8,4,160,128]{3,2,1,0:T(8,128)(2,1)}, u32[]{:S(2)}) copy-start(bf16[8,4,160,128]{3,2,1,0:T(8,128)(2,1)} %param.9) | copy-start | bytes 3932164
  102.5 23.8 %copy-start.4 = (bf16[8,4,160,128]{3,2,1,0:T(8,128)(2,1)}, bf16[8,4,160,128]{3,2,1,0:T(8,128)(2,1)S(1)}, u32[]{:S(2)}) copy-start(bf16[8,4,160,128]{3,2,1,0:T(8,128)(2,1)S(1)} %fusion.19) | copy-start | bytes 3932164
  102.5 10.4 %collective-permute-start.8 = (bf16[1,4,160,128]{3,2,1,0:T(8,128)(2,1)S(1)}, bf16[1,4,160,128]{3,2,1,0:T(8,128)(2,1)S(1)}, u32[]{:S(2)}, u32[]{:S(2)}) collective-permute-start(bf16[1,4,160,128]{3,2,1,0:T(8,128)(2,1)S(1)} %get-tuple-element.16), channel_id=1, source_target_pairs={{0,4},{4,8},{8,12},{12,16},{16,20},{20,24},{24,28},{28,32},{32,36}... | collective-permute-start | bytes 491528 | tf_op jit(solution)/shard_map/ppermute | solution.py:16
  102.6 10.3 %collective-permute-start.9 = (bf16[1,4,160,128]{3,2,1,0:T(8,128)(2,1)S(1)}, bf16[1,4,160,128]{3,2,1,0:T(8,128)(2,1)S(1)}, u32[]{:S(2)}, u32[]{:S(2)}) collective-permute-start(bf16[1,4,160,128]{3,2,1,0:T(8,128)(2,1)S(1)} %get-tuple-element.17), channel_id=1, source_target_pairs={{4,0},{8,4},{12,8},{16,12},{20,16},{24,20},{28,24},{32,28},{36,32}... | collective-permute-start | bytes 491528 | tf_op jit(solution)/shard_map/ppermute | solution.py:19
  113.0 11.4 %collective-permute-start.10 = (bf16[10,1,160,128]{3,2,1,0:T(8,128)(2,1)S(1)}, bf16[10,1,160,128]{3,2,1,0:T(8,128)(2,1)S(1)}, u32[]{:S(2)}, u32[]{:S(2)}) collective-permute-start(bf16[10,1,160,128]{3,2,1,0:T(8,128)(2,1)S(1)} %get-tuple-element.8), channel_id=1, source_target_pairs={{0,1},{1,2},{2,3},{3,0},{4,5},{5,6},{6,7},{7,4},{8,9},{9,10},{10,1... | collective-permute-start | bytes 1228808 | tf_op jit(solution)/shard_map/ppermute | solution.py:16
  116.3 10.0 %collective-permute-start.11 = (bf16[10,1,160,128]{3,2,1,0:T(8,128)(2,1)S(1)}, bf16[10,1,160,128]{3,2,1,0:T(8,128)(2,1)S(1)}, u32[]{:S(2)}, u32[]{:S(2)}) collective-permute-start(bf16[10,1,160,128]{3,2,1,0:T(8,128)(2,1)S(1)} %get-tuple-element.9), channel_id=1, source_target_pairs={{1,0},{2,1},{3,2},{0,3},{5,4},{6,5},{7,6},{4,7},{9,8},{10,9},{11,1... | collective-permute-start | bytes 1228808 | tf_op jit(solution)/shard_map/ppermute | solution.py:19
  135.7 8.4 %copy-start.3 = (bf16[8,4,160,128]{3,2,1,0:T(8,128)(2,1)S(1)}, bf16[8,4,160,128]{3,2,1,0:T(8,128)(2,1)}, u32[]{:S(2)}) copy-start(bf16[8,4,160,128]{3,2,1,0:T(8,128)(2,1)} %copy-done.2) | copy-start | bytes 3932164
  135.7 8.4 %copy-start.5 = (bf16[8,4,160,128]{3,2,1,0:T(8,128)(2,1)S(1)}, bf16[8,4,160,128]{3,2,1,0:T(8,128)(2,1)}, u32[]{:S(2)}) copy-start(bf16[8,4,160,128]{3,2,1,0:T(8,128)(2,1)} %copy-done.4) | copy-start | bytes 3932164
  144.8 44.3 %copy-start.1 = (bf16[8,4,160,128]{3,2,1,0:T(8,128)(2,1)}, bf16[8,4,160,128]{3,2,1,0:T(8,128)(2,1)S(1)}, u32[]{:S(2)}) copy-start(bf16[8,4,160,128]{3,2,1,0:T(8,128)(2,1)S(1)} %fusion.22) | copy-start | bytes 3932164
  144.9 10.5 %collective-permute-start.12 = (bf16[1,4,160,128]{3,2,1,0:T(8,128)(2,1)S(1)}, bf16[1,4,160,128]{3,2,1,0:T(8,128)(2,1)S(1)}, u32[]{:S(2)}, u32[]{:S(2)}) collective-permute-start(bf16[1,4,160,128]{3,2,1,0:T(8,128)(2,1)S(1)} %get-tuple-element.14), channel_id=1, source_target_pairs={{0,4},{4,8},{8,12},{12,16},{16,20},{20,24},{24,28},{28,32},{32,36}... | collective-permute-start | bytes 491528 | tf_op jit(solution)/shard_map/ppermute | solution.py:16
  144.9 10.4 %collective-permute-start.13 = (bf16[1,4,160,128]{3,2,1,0:T(8,128)(2,1)S(1)}, bf16[1,4,160,128]{3,2,1,0:T(8,128)(2,1)S(1)}, u32[]{:S(2)}, u32[]{:S(2)}) collective-permute-start(bf16[1,4,160,128]{3,2,1,0:T(8,128)(2,1)S(1)} %get-tuple-element.15), channel_id=1, source_target_pairs={{4,0},{8,4},{12,8},{16,12},{20,16},{24,20},{28,24},{32,28},{36,32}... | collective-permute-start | bytes 491528 | tf_op jit(solution)/shard_map/ppermute | solution.py:19
  155.4 11.5 %collective-permute-start.14 = (bf16[10,1,160,128]{3,2,1,0:T(8,128)(2,1)S(1)}, bf16[10,1,160,128]{3,2,1,0:T(8,128)(2,1)S(1)}, u32[]{:S(2)}, u32[]{:S(2)}) collective-permute-start(bf16[10,1,160,128]{3,2,1,0:T(8,128)(2,1)S(1)} %get-tuple-element.6), channel_id=1, source_target_pairs={{0,1},{1,2},{2,3},{3,0},{4,5},{5,6},{6,7},{7,4},{8,9},{9,10},{10,1... | collective-permute-start | bytes 1228808 | tf_op jit(solution)/shard_map/ppermute | solution.py:16
  158.7 10.0 %collective-permute-start.15 = (bf16[10,1,160,128]{3,2,1,0:T(8,128)(2,1)S(1)}, bf16[10,1,160,128]{3,2,1,0:T(8,128)(2,1)S(1)}, u32[]{:S(2)}, u32[]{:S(2)}) collective-permute-start(bf16[10,1,160,128]{3,2,1,0:T(8,128)(2,1)S(1)} %get-tuple-element.7), channel_id=1, source_target_pairs={{1,0},{2,1},{3,2},{0,3},{5,4},{6,5},{7,6},{4,7},{9,8},{10,9},{11,1... | collective-permute-start | bytes 1228808 | tf_op jit(solution)/shard_map/ppermute | solution.py:19
Sparse Core Ops, SparseCore 0:
  190.5 248.8 all-reduce.2
where the time goes:
time: 457 us; the launch traced here: 448 us
  waiting for transfers between devices  296 us (65%)
  matrix products  43.8 us (10%)
  starting transfers between devices  41.6 us (9%)
  local copies, waits for them, and re-layouts  40.6 us (9%)
  between operations  14.8 us (3%)
  other arithmetic  11.2 us (2%)
    psum x1, waiting for transfers between devices, on_device(): gram_total, ritz_total = lax.psum((gram_part, ritz_part), ('elem', 'band'))  249 us
    ppermute x8, waiting for transfers between devices, extended_2(): lax.ppermute(lax.slice_in_dim(block, block.shape[dim] - width, None, axis...  40.3 us
    gather x4, local copies, waits for them, and re-layouts, apply_op(): nearby = jnp.take(extended, gather_index, axis=0)  39.1 us
    dot_general x4, matrix products, apply_op(): jnp.einsum('ekcs,eksr->ecr', nearby, near_flat, preferred_element_type=jn...  33.1 us
    ppermute x8, starting transfers between devices, extended_2(): lax.ppermute(lax.slice_in_dim(block, 0, width, axis=dim), axis, backward)  25.4 us
    ppermute x8, starting transfers between devices, extended_2(): lax.ppermute(lax.slice_in_dim(block, block.shape[dim] - width, None, axis...  16.1 us
  transfers between devices with their start and end apart: 17, of which 13 were waited for; matrix products, arithmetic and copies ran while one was open for 2% of the time, Pallas kernels for 0%

commit v1 on v0

v1 whole, which is shorter than its diff:
```python
import functools

import jax
import jax.numpy as jnp
from jax import lax
from jax.experimental import pallas as pl
from jax.experimental.pallas import tpu as pltpu
from jax.sharding import Mesh, PartitionSpec as P

CENTER = 0.25
INV_HALF = 1.0 / 1.5
ANY = pl.BlockSpec(memory_space=pl.ANY)


def nt_dot(a, b):
    return lax.dot_general(a, b, (((1,), (1,)), ((), ())), preferred_element_type=jnp.float32)


def step_kernel(mode, dims, index_ref, count_ref, band_ref, *refs):
    rows, cols, columns, basis, neighbours = dims
    wide = cols + 2
    refs = list(refs)
    x_hbm, low_hbm, high_hbm, left_hbm, right_hbm, corner_low, corner_high = refs[:7]
    self_ref, near_ref = refs[7:9]
    del refs[:9]
    prev_ref = refs.pop(0) if mode in ("second", "third") else None
    gram_in = refs.pop(0) if mode == "image" else None
    out_ref = refs.pop(0) if mode != "image" else None
    gram_ref = refs.pop(0) if mode == "third" else None
    pieces = [refs.pop(0) for _ in range(4)] if mode == "image" else None
    ext, sem = refs[:2]
    acc = refs[2] if mode == "image" else None
    i = pl.program_id(0)

    @pl.when(i == 0)
    def _():
        copies = []

        def move(src, slot, count):
            copies.append(pltpu.make_async_copy(src, ext.at[pl.ds(slot, count)], sem))

        for r in range(rows):
            move(x_hbm.at[r], (r + 1) * wide + 1, cols)
            move(left_hbm.at[r], (r + 1) * wide, 1)
            move(right_hbm.at[r], (r + 1) * wide + wide - 1, 1)
        move(low_hbm.at[0], 1, cols)
        move(high_hbm.at[0], (rows + 1) * wide + 1, cols)
        move(corner_low.at[0, pl.ds(0, 1)], 0, 1)
        move(corner_low.at[0, pl.ds(1, 1)], wide - 1, 1)
        move(corner_high.at[0, pl.ds(0, 1)], (rows + 1) * wide, 1)
        move(corner_high.at[0, pl.ds(1, 1)], (rows + 2) * wide - 1, 1)
        for c in copies:
            c.start()
        for c in copies:
            c.wait()
        if mode == "third":
            gram_ref[...] = jnp.zeros_like(gram_ref)
        if mode == "image":
            acc[...] = jnp.zeros_like(acc)

    lane = lax.broadcasted_iota(jnp.int32, (columns, basis), 1)
    made, held = [], []
    for j in range(cols):
        own = ext[(i + 1) * wide + j + 1]
        tiles = [ext[index_ref[i, j * neighbours + k]] for k in range(neighbours)]
        weights = near_ref[0, j]
        total = None
        for k in range(0, neighbours, 2):
            lhs = jnp.concatenate([tiles[k], tiles[k + 1]], axis=1)
            rhs = weights[k : k + 2].reshape(2 * basis, basis)
            part = jnp.dot(lhs, rhs, preferred_element_type=jnp.float32)
            total = part if total is None else total + part
        total = total + jnp.dot(own, self_ref[0, j], preferred_element_type=jnp.float32)
        live = lane < count_ref[i, j]
        total = jnp.where(live, total, 0.0)
        if mode != "image":
            value = (total - CENTER * own.astype(jnp.float32)) * INV_HALF
            if mode != "first":
                value = 2.0 * value - prev_ref[0, j].astype(jnp.float32)
            total = value
        result = total.astype(jnp.bfloat16)
        if mode != "image":
            out_ref[0, j] = result
        made.append(result)
        held.append(own)
    if mode == "third":
        wide_f = jnp.concatenate(made, axis=1)
        gram_ref[...] += nt_dot(wide_f, wide_f)
    if mode == "image":
        acc[...] += nt_dot(jnp.concatenate(held, axis=1), jnp.concatenate(made, axis=1))

        @pl.when(i == rows - 1)
        def _():
            share = columns // 4
            for s in range(4):
                first = pl.multiple_of(lax.rem(band_ref[0] + s, 4) * share, 8)
                pieces[s][0] = gram_in[pl.ds(first, share), :]
                pieces[s][1] = acc[pl.ds(first, share), :]


def apply_step(mode, x, halo, index, counts, band, h_self, h_near, prev=None, gram=None):
    rows, cols, columns, basis = x.shape
    neighbours = h_near.shape[2]
    dims = (rows, cols, columns, basis, neighbours)
    row = lambda i, *_: (i, 0, 0, 0)
    row5 = lambda i, *_: (i, 0, 0, 0, 0)
    fixed = lambda i, *_: (0, 0)
    in_specs = [ANY] * 7 + [
        pl.BlockSpec((1, cols, basis, basis), row),
        pl.BlockSpec((1, cols, neighbours, basis, basis), row5),
    ]
    args = [x, *halo, h_self, h_near]
    square = jax.ShapeDtypeStruct((columns, columns), jnp.float32)
    square_spec = pl.BlockSpec((columns, columns), fixed)
    scratch = [
        pltpu.VMEM(((rows + 2) * (cols + 2), columns, basis), jnp.bfloat16),
        pltpu.SemaphoreType.DMA,
    ]
    if prev is not None:
        in_specs.append(pl.BlockSpec((1, cols, columns, basis), row))
        args.append(prev)
    if mode == "image":
        in_specs.append(square_spec)
        args.append(gram)
        piece = (2, columns // 4, columns)
        out_shape = [jax.ShapeDtypeStruct(piece, jnp.float32)] * 4
        out_specs = [pl.BlockSpec(piece, lambda i, *_: (0, 0, 0))] * 4
        scratch.append(pltpu.VMEM((columns, columns), jnp.float32))
    else:
        out_shape = [jax.ShapeDtypeStruct(x.shape, jnp.bfloat16)]
        out_specs = [pl.BlockSpec((1, cols, columns, basis), row)]
        if mode == "third":
            out_shape.append(square)
            out_specs.append(square_spec)
    flops = 2 * rows * cols * columns * basis * basis * (neighbours + 1)
    return pl.pallas_call(
        functools.partial(step_kernel, mode, dims),
        out_shape=out_shape,
        grid_spec=pltpu.PrefetchScalarGridSpec(
            num_scalar_prefetch=3,
            grid=(rows,),
            in_specs=in_specs,
            out_specs=out_specs,
            scratch_shapes=scratch,
        ),
        compiler_params=pltpu.CompilerParams(
            dimension_semantics=("arbitrary",), vmem_limit_bytes=24 * 1024 * 1024
        ),
        cost_estimate=pl.CostEstimate(flops=flops, bytes_accessed=10_000_000, transcendentals=0),
        name="step_" + mode,
    )(index, counts, band, *args)


def shifted(value, axes, count, step):
    return lax.ppermute(value, axes, [(p, (p + step) % count) for p in range(count)])


def on_device(elem, band, sizes, basis_counts, neighbour_codes, x_block, h_self, h_near):
    rows, cols, columns, basis = x_block.shape
    neighbours = neighbour_codes.shape[2]
    wide = cols + 2
    n_elem, n_band = sizes
    row_iota = lax.broadcasted_iota(jnp.int32, (rows, cols, neighbours), 0)
    col_iota = lax.broadcasted_iota(jnp.int32, (rows, cols, neighbours), 1)
    index = (
        (row_iota + neighbour_codes // 3) * wide + col_iota + neighbour_codes % 3
    ).reshape(rows, cols * neighbours)
    band_at = lax.axis_index(band).astype(jnp.int32)
    live = lax.broadcasted_iota(jnp.int32, x_block.shape, 3) < basis_counts[:, :, None, None]
    start = jnp.where(live, x_block, jnp.zeros_like(x_block))

    def exchange(v):
        left = shifted(v[:, cols - 1 :], band, n_band, 1)
        right = shifted(v[:, :1], band, n_band, -1)
        low = shifted(v[rows - 1 :], elem, n_elem, 1)
        high = shifted(v[:1], elem, n_elem, -1)
        edge_low = jnp.concatenate([left[rows - 1 :], right[rows - 1 :]], axis=1)
        edge_high = jnp.concatenate([left[:1], right[:1]], axis=1)
        corner_low = shifted(edge_low, elem, n_elem, 1)
        corner_high = shifted(edge_high, elem, n_elem, -1)
        return low, high, left, right, corner_low, corner_high

    def apply(mode, v, **more):
        return apply_step(
            mode, v, exchange(v), index, basis_counts, band_at.reshape(1), h_self, h_near, **more
        )

    (first,) = apply("first", start)
    (second,) = apply("second", first, prev=start)
    filtered, gram = apply("third", second, prev=first)
    pieces = apply("image", filtered, gram=gram)
    total = pieces[0]
    for s in range(1, n_band):
        total = total + shifted(pieces[s], band, n_band, s)

    def fold(value, axis, maps):
        moved = [lax.ppermute(value, axis, pairs) for pairs in maps]
        return sum(moved, value)

    total = fold(total, "x", [[(p, (p + s) % 4) for p in range(4)] for s in (1, 2, 3)])
    total = fold(total, "yl", [[(p, 1 - p) for p in range(2)]])
    for pairs in ([(p, p ^ 1) for p in range(8)], [(p, p ^ 2) for p in range(8)], [(p, 7 - p) for p in range(8)]):
        total = fold(total, "z", [pairs])
    normalizer = jnp.float32(rows * cols * n_elem * n_band * basis / 3.0)
    total = total / normalizer
    return filtered, total[0], total[1]


def solution(mesh):
    split = Mesh(mesh.devices.reshape(8, 2, 4, 2, 2), ("z", "yl", "x", "yh", "core"))
    elem, band = ("z", "yl", "x"), ("yh", "core")
    in_specs = (P(elem, band),) + tuple(P(elem, band, *[None] * n) for n in (1, 2, 2, 3))
    out_specs = (P(elem, band, None, None), P(band, None), P(band, None))
    body = functools.partial(on_device, elem, band, (64, 4))
    return jax.shard_map(body, mesh=split, in_specs=in_specs, out_specs=out_specs, check_vma=False)
```

time: 457 us -> 191 us (0.42)
  the two profiles are of different devices: /device:TPU:1 before, /device:TPU:40 now
where the time goes in v1:
time: 191 us; the launch traced here: 190 us
  starting transfers between devices  81.9 us (43%)
  waiting for transfers between devices  58 us (30%)
  Pallas kernels  35.1 us (18%)
  local copies, waits for them, and re-layouts  11.2 us (6%)
  other arithmetic  3.25 us (2%)
    ppermute x27, starting transfers between devices, shifted(): lax.ppermute(value, axes, [(p, (p + step) % count) for p in range(count)])  57.6 us
    pallas_call x4, Pallas kernels, apply_step(): pl.pallas_call(functools.partial(step_kernel, mode, dims), out_shape=out_...  35.1 us
    ppermute x27, waiting for transfers between devices, shifted(): lax.ppermute(value, axes, [(p, (p + step) % count) for p in range(count)])  32.3 us
    ppermute x7, waiting for transfers between devices, fold(): moved = [lax.ppermute(value, axis, pairs) for pairs in maps]  25.8 us
    ppermute x7, starting transfers between devices, fold(): moved = [lax.ppermute(value, axis, pairs) for pairs in maps]  24.2 us
    unnamed x21, local copies, waits for them, and re-layouts  8.17 us
  transfers between devices with their start and end apart: 34, of which 24 were waited for; matrix products, arithmetic and copies ran while one was open for 1% of the time, Pallas kernels for 0%

profile of v1, /device:TPU:40, one launch (start us, length us, event | category | flops | bytes accessed | tf_op | source)
XLA Modules:
  0.0 190.3 jit_solution(8932839949016558164)
XLA Ops:
  5.8 3.5 %collective-permute-start.1 = (bf16[1,4,160,128]{3,2,1,0:T(8,128)(2,1)}, bf16[1,4,160,128]{3,2,1,0:T(8,128)(2,1)}, u32[]{:S(2)}, u32[]{:S(2)}) collective-permute-start(bf16[1,4,160,128]{3,2,1,0:T(8,128)(2,1)} %get-tuple-element.29), channel_id=1, source_target_pairs={{0,252},{4,0},{8,4},{12,8},{16,12},{20,16},{24,20},{28,24},{32,28}... | collective-permute-start | bytes 491528 | tf_op jit(solution)/shard_map/ppermute | solution.py:155
  9.4 3.1 %collective-permute-done.3.refs_4_ = bf16[8,1,160,128]{3,2,1,0:T(8,128)(2,1)S(1)} collective-permute-done((bf16[8,1,160,128]{3,2,1,0:T(8,128)(2,1)S(1)}, bf16[8,1,160,128]{3,2,1,0:T(8,128)(2,1)S(1)}, u32[]{:S(2)}, u32[]{:S(2)}) %collective-permute-start.3) | collective-permute-done | bytes 327712 | tf_op jit(solution)/shard_map/ppermute | solution.py:155
  18.4 4.9 %collective-permute-start.5 = (bf16[1,2,160,128]{3,2,1,0:T(8,128)(2,1)}, bf16[1,2,160,128]{3,2,1,0:T(8,128)(2,1)}, u32[]{:S(2)}, u32[]{:S(2)}) collective-permute-start(bf16[1,2,160,128]{3,2,1,0:T(8,128)(2,1)} %pad_maximum_fusion.1), channel_id=1, source_target_pairs={{0,252},{4,0},{8,4},{12,8},{16,12},{20,16},{24,20},{28,24},{32,28}... | collective-permute-start | bytes 245768 | tf_op jit(solution)/shard_map/ppermute | solution.py:155
  25.6 2.8 %copy-done = bf16[8,4,6,128,128]{4,3,2,1,0:T(8,128)(2,1)S(1)} copy-done((bf16[8,4,6,128,128]{4,3,2,1,0:T(8,128)(2,1)S(1)}, bf16[8,4,6,128,128]{4,3,2,1,0:T(8,128)(2,1)}, u32[]{:S(2)}) %copy-start) | copy-done | bytes 6291480
  31.6 8.0 %step_first.1.refs_0_.refs_9_ = bf16[8,4,160,128]{3,2,1,0:T(8,128)(2,1)S(1)} custom-call(s32[8,24]{1,0:T(8,128)S(1)} %reshape.16.index_ref, s32[8,4]{1,0:T(8,128)S(1)} %copy.18.count_ref, s32[1]{0:T(128)} %bitcast.band_ref, bf16[8,4,160,128]{3,2,1,0:T(8,128)(2,1)S(1)} %fusion.refs_0_.refs_9_, bf16[1,4,160,128]{3,2,1,0:T(8,128)(2,1)} %collective-permute-done.refs_1_, ...), custom_call_target="tpu_custom_call" | custom-call | flops 1174405120 | bytes 10000000 | tf_op jit(solution)/shard_map/step_first/pallas_call | solution.py:136
  39.6 2.5 %collective-permute-start.9 = (bf16[8,1,160,128]{3,2,1,0:T(8,128)(2,1)S(1)}, bf16[8,1,160,128]{3,2,1,0:T(8,128)(2,1)S(1)}, u32[]{:S(2)}, u32[]{:S(2)}) collective-permute-start(bf16[8,1,160,128]{3,2,1,0:T(8,128)(2,1)S(1)} %get-tuple-element.23), channel_id=1, source_target_pairs={{0,3},{1,0},{2,1},{3,2},{4,7},{5,4},{6,5},{7,6},{8,11},{9,8},{10,9... | collective-permute-start | bytes 983048 | tf_op jit(solution)/shard_map/ppermute | solution.py:155
  42.2 5.2 %collective-permute-start.7 = (bf16[1,4,160,128]{3,2,1,0:T(8,128)(2,1)S(1)}, bf16[1,4,160,128]{3,2,1,0:T(8,128)(2,1)S(1)}, u32[]{:S(2)}, u32[]{:S(2)}) collective-permute-start(bf16[1,4,160,128]{3,2,1,0:T(8,128)(2,1)S(1)} %get-tuple-element.25), channel_id=1, source_target_pairs={{0,252},{4,0},{8,4},{12,8},{16,12},{20,16},{24,20},{28,24},{32,28}... | collective-permute-start | bytes 491528 | tf_op jit(solution)/shard_map/ppermute | solution.py:155
  47.5 2.8 %collective-permute-done.9.refs_4_ = bf16[8,1,160,128]{3,2,1,0:T(8,128)(2,1)S(1)} collective-permute-done((bf16[8,1,160,128]{3,2,1,0:T(8,128)(2,1)S(1)}, bf16[8,1,160,128]{3,2,1,0:T(8,128)(2,1)S(1)}, u32[]{:S(2)}, u32[]{:S(2)}) %collective-permute-start.9) | collective-permute-done | bytes 327712 | tf_op jit(solution)/shard_map/ppermute | solution.py:155
  52.4 6.8 %collective-permute-start.11 = (bf16[1,2,160,128]{3,2,1,0:T(8,128)(2,1)S(1)}, bf16[1,2,160,128]{3,2,1,0:T(8,128)(2,1)S(1)}, u32[]{:S(2)}, u32[]{:S(2)}) collective-permute-start(bf16[1,2,160,128]{3,2,1,0:T(8,128)(2,1)S(1)} %pad_maximum_fusion.3), channel_id=1, source_target_pairs={{0,252},{4,0},{8,4},{12,8},{16,12},{20,16},{24,20},{28,24},{32,28}... | collective-permute-start | bytes 245768 | tf_op jit(solution)/shard_map/ppermute | solution.py:155
  59.2 2.4 %collective-permute-done.10.refs_5_ = bf16[1,2,160,128]{3,2,1,0:T(8,128)(2,1)S(1)} collective-permute-done((bf16[1,2,160,128]{3,2,1,0:T(8,128)(2,1)S(1)}, bf16[1,2,160,128]{3,2,1,0:T(8,128)(2,1)S(1)}, u32[]{:S(2)}, u32[]{:S(2)}) %collective-permute-start.10) | collective-permute-done | bytes 81952 | tf_op jit(solution)/shard_map/ppermute | solution.py:155
  61.7 7.6 %step_second.1.refs_0_ = bf16[8,4,160,128]{3,2,1,0:T(8,128)(2,1)S(1)} custom-call(s32[8,24]{1,0:T(8,128)S(1)} %reshape.16.index_ref, s32[8,4]{1,0:T(8,128)S(1)} %copy.18.count_ref, s32[1]{0:T(128)} %bitcast.band_ref, bf16[8,4,160,128]{3,2,1,0:T(8,128)(2,1)S(1)} %step_first.1.refs_0_.refs_9_, bf16[1,4,160,128]{3,2,1,0:T(8,128)(2,1)S(1)} %collective-permute-done.6.refs_1_, ...), custom_call_target="tpu_custom_call" | custom-call | flops 1174405120 | bytes 10000000 | tf_op jit(solution)/shard_map/step_second/pallas_call | solution.py:136
  69.4 2.8 %collective-permute-start.15 = (bf16[8,1,160,128]{3,2,1,0:T(8,128)(2,1)S(1)}, bf16[8,1,160,128]{3,2,1,0:T(8,128)(2,1)S(1)}, u32[]{:S(2)}, u32[]{:S(2)}) collective-permute-start(bf16[8,1,160,128]{3,2,1,0:T(8,128)(2,1)S(1)} %get-tuple-element.19), channel_id=1, source_target_pairs={{0,3},{1,0},{2,1},{3,2},{4,7},{5,4},{6,5},{7,6},{8,11},{9,8},{10,9... | collective-permute-start | bytes 983048 | tf_op jit(solution)/shard_map/ppermute | solution.py:155
  72.2 4.3 %collective-permute-start.13 = (bf16[1,4,160,128]{3,2,1,0:T(8,128)(2,1)S(1)}, bf16[1,4,160,128]{3,2,1,0:T(8,128)(2,1)S(1)}, u32[]{:S(2)}, u32[]{:S(2)}) collective-permute-start(bf16[1,4,160,128]{3,2,1,0:T(8,128)(2,1)S(1)} %get-tuple-element.21), channel_id=1, source_target_pairs={{0,252},{4,0},{8,4},{12,8},{16,12},{20,16},{24,20},{28,24},{32,28}... | collective-permute-start | bytes 491528 | tf_op jit(solution)/shard_map/ppermute | solution.py:155
  76.5 3.2 %collective-permute-done.15.refs_4_ = bf16[8,1,160,128]{3,2,1,0:T(8,128)(2,1)S(1)} collective-permute-done((bf16[8,1,160,128]{3,2,1,0:T(8,128)(2,1)S(1)}, bf16[8,1,160,128]{3,2,1,0:T(8,128)(2,1)S(1)}, u32[]{:S(2)}, u32[]{:S(2)}) %collective-permute-start.15) | collective-permute-done | bytes 327712 | tf_op jit(solution)/shard_map/ppermute | solution.py:155
  81.6 3.4 %collective-permute-start.16 = (bf16[1,2,160,128]{3,2,1,0:T(8,128)(2,1)S(1)}, bf16[1,2,160,128]{3,2,1,0:T(8,128)(2,1)S(1)}, u32[]{:S(2)}, u32[]{:S(2)}) collective-permute-start(bf16[1,2,160,128]{3,2,1,0:T(8,128)(2,1)S(1)} %pad_maximum_fusion.4), channel_id=1, source_target_pairs={{0,4},{4,8},{8,12},{12,16},{16,20},{20,24},{24,28},{28,32},{32,36}... | collective-permute-start | bytes 245768 | tf_op jit(solution)/shard_map/ppermute | solution.py:155
  86.3 2.3 %collective-permute-done.16.refs_5_ = bf16[1,2,160,128]{3,2,1,0:T(8,128)(2,1)S(1)} collective-permute-done((bf16[1,2,160,128]{3,2,1,0:T(8,128)(2,1)S(1)}, bf16[1,2,160,128]{3,2,1,0:T(8,128)(2,1)S(1)}, u32[]{:S(2)}, u32[]{:S(2)}) %collective-permute-start.16) | collective-permute-done | bytes 81952 | tf_op jit(solution)/shard_map/ppermute | solution.py:155
  89.6 10.1 %step_third.1 = (bf16[8,4,160,128]{3,2,1,0:T(8,128)(2,1)}, f32[160,160]{1,0:T(8,128)S(1)}) custom-call(s32[8,24]{1,0:T(8,128)S(1)} %reshape.16.index_ref, s32[8,4]{1,0:T(8,128)S(1)} %copy.18.count_ref, s32[1]{0:T(128)} %bitcast.band_ref, bf16[8,4,160,128]{3,2,1,0:T(8,128)(2,1)S(1)} %step_second.1.refs_0_, ...), custom_call_target="tpu_custom_call" | custom-call | flops 1174405120 | bytes 10000000 | tf_op jit(solution)/shard_map/step_third/pallas_call | solution.py:136
  101.5 3.9 %collective-permute-start.19 = (bf16[1,4,160,128]{3,2,1,0:T(8,128)(2,1)S(1)}, bf16[1,4,160,128]{3,2,1,0:T(8,128)(2,1)S(1)}, u32[]{:S(2)}, u32[]{:S(2)}) collective-permute-start(bf16[1,4,160,128]{3,2,1,0:T(8,128)(2,1)S(1)} %get-tuple-element.17), channel_id=1, source_target_pairs={{0,252},{4,0},{8,4},{12,8},{16,12},{20,16},{24,20},{28,24},{32,28}... | collective-permute-start | bytes 491528 | tf_op jit(solution)/shard_map/ppermute | solution.py:155
  105.4 3.7 %collective-permute-start.18 = (bf16[1,4,160,128]{3,2,1,0:T(8,128)(2,1)S(1)}, bf16[1,4,160,128]{3,2,1,0:T(8,128)(2,1)S(1)}, u32[]{:S(2)}, u32[]{:S(2)}) collective-permute-start(bf16[1,4,160,128]{3,2,1,0:T(8,128)(2,1)S(1)} %get-tuple-element.18), channel_id=1, source_target_pairs={{0,4},{4,8},{8,12},{12,16},{16,20},{20,24},{24,28},{28,32},{32,36}... | collective-permute-start | bytes 491528 | tf_op jit(solution)/shard_map/ppermute | solution.py:155
  109.1 4.4 %collective-permute-done.20.refs_3_ = bf16[8,1,160,128]{3,2,1,0:T(8,128)(2,1)S(1)} collective-permute-done((bf16[8,1,160,128]{3,2,1,0:T(8,128)(2,1)S(1)}, bf16[8,1,160,128]{3,2,1,0:T(8,128)(2,1)S(1)}, u32[]{:S(2)}, u32[]{:S(2)}) %collective-permute-start.20) | collective-permute-done | bytes 327712 | tf_op jit(solution)/shard_map/ppermute | solution.py:155
  113.5 5.3 %collective-permute-start.22 = (bf16[1,2,160,128]{3,2,1,0:T(8,128)(2,1)S(1)}, bf16[1,2,160,128]{3,2,1,0:T(8,128)(2,1)S(1)}, u32[]{:S(2)}, u32[]{:S(2)}) collective-permute-start(bf16[1,2,160,128]{3,2,1,0:T(8,128)(2,1)S(1)} %pad_maximum_fusion.6), channel_id=1, source_target_pairs={{0,4},{4,8},{8,12},{12,16},{16,20},{20,24},{24,28},{28,32},{32,36}... | collective-permute-start | bytes 245768 | tf_op jit(solution)/shard_map/ppermute | solution.py:155
  119.0 2.3 %collective-permute-done.22.refs_5_ = bf16[1,2,160,128]{3,2,1,0:T(8,128)(2,1)S(1)} collective-permute-done((bf16[1,2,160,128]{3,2,1,0:T(8,128)(2,1)S(1)}, bf16[1,2,160,128]{3,2,1,0:T(8,128)(2,1)S(1)}, u32[]{:S(2)}, u32[]{:S(2)}) %collective-permute-start.22) | collective-permute-done | bytes 81952 | tf_op jit(solution)/shard_map/ppermute | solution.py:155
  123.4 9.4 %step_image.1 = (f32[2,40,160]{2,1,0:T(8,128)S(1)}, f32[2,40,160]{2,1,0:T(8,128)S(1)}, f32[2,40,160]{2,1,0:T(8,128)S(1)}, f32[2,40,160]{2,1,0:T(8,128)S(1)}) custom-call(s32[8,24]{1,0:T(8,128)S(1)} %reshape.16.index_ref, s32[8,4]{1,0:T(8,128)S(1)} %copy.18.count_ref, s32[1]{0:T(128)} %bitcast.band_ref, bf16[8,4,160,128]{3,2,1,0:T(8,128)(2,1)S(1)} %copy-done.2, ...), custom_call_target="tpu_custom_call" | custom-call | flops 1174405120 | bytes 10000000 | tf_op jit(solution)/shard_map/step_image/pallas_call | solution.py:136
  134.6 2.9 %collective-permute-start.26 = (f32[2,40,160]{2,1,0:T(8,128)S(1)}, f32[2,40,160]{2,1,0:T(8,128)S(1)}, u32[]{:S(2)}, u32[]{:S(2)}) collective-permute-start(f32[2,40,160]{2,1,0:T(8,128)S(1)} %get-tuple-element.14), channel_id=1, source_target_pairs={{0,3},{1,0},{2,1},{3,2},{4,7},{5,4},{6,5},{7,6},{8,11},{9,8},{10,9... | collective-permute-start | bytes 153608 | tf_op jit(solution)/shard_map/ppermute | solution.py:155
  139.6 14.1 %collective-permute-start.29 = (f32[2,40,160]{2,1,0:T(8,128)S(1)}, f32[2,40,160]{2,1,0:T(8,128)S(1)}, u32[]{:S(2)}, u32[]{:S(2)}) collective-permute-start(f32[2,40,160]{2,1,0:T(8,128)S(1)} %add_add_fusion.1), channel_id=1, source_target_pairs={{0,12},{4,0},{8,4},{12,8},{1,13},{5,1},{9,5},{13,9},{2,14},{6,2},{... | collective-permute-start | bytes 153608 | tf_op jit(solution)/shard_map/ppermute | solution.py:197
  154.6 3.0 %collective-permute-done.29 = f32[2,40,160]{2,1,0:T(8,128)S(1)} collective-permute-done((f32[2,40,160]{2,1,0:T(8,128)S(1)}, f32[2,40,160]{2,1,0:T(8,128)S(1)}, u32[]{:S(2)}, u32[]{:S(2)}) %collective-permute-start.29) | collective-permute-done | bytes 51232 | tf_op jit(solution)/shard_map/ppermute | solution.py:197
  157.6 2.4 %collective-permute-done.28 = f32[2,40,160]{2,1,0:T(8,128)S(1)} collective-permute-done((f32[2,40,160]{2,1,0:T(8,128)S(1)}, f32[2,40,160]{2,1,0:T(8,128)S(1)}, u32[]{:S(2)}, u32[]{:S(2)}) %collective-permute-start.28) | collective-permute-done | bytes 51232 | tf_op jit(solution)/shard_map/ppermute | solution.py:197
  161.7 4.5 %collective-permute-done.30 = f32[2,40,160]{2,1,0:T(8,128)S(1)} collective-permute-done((f32[2,40,160]{2,1,0:T(8,128)S(1)}, f32[2,40,160]{2,1,0:T(8,128)S(1)}, u32[]{:S(2)}, u32[]{:S(2)}) %collective-permute-start.30) | collective-permute-done | bytes 51232 | tf_op jit(solution)/shard_map/ppermute | solution.py:197
  166.4 4.4 %collective-permute-done.31 = f32[2,40,160]{2,1,0:T(8,128)S(1)} collective-permute-done((f32[2,40,160]{2,1,0:T(8,128)S(1)}, f32[2,40,160]{2,1,0:T(8,128)S(1)}, u32[]{:S(2)}, u32[]{:S(2)}) %collective-permute-start.31) | collective-permute-done | bytes 51232 | tf_op jit(solution)/shard_map/ppermute | solution.py:197
  170.8 8.9 %collective-permute-start.32 = (f32[2,40,160]{2,1,0:T(8,128)S(1)}, f32[2,40,160]{2,1,0:T(8,128)S(1)}, u32[]{:S(2)}, u32[]{:S(2)}) collective-permute-start(f32[2,40,160]{2,1,0:T(8,128)S(1)} %add.61), channel_id=1, source_target_pairs={{0,64},{32,96},{64,0},{96,32},{128,192},{160,224},{192,128},{224,1... | collective-permute-start | bytes 153608 | tf_op jit(solution)/shard_map/ppermute | solution.py:197
  179.7 2.4 %collective-permute-done.32 = f32[2,40,160]{2,1,0:T(8,128)S(1)} collective-permute-done((f32[2,40,160]{2,1,0:T(8,128)S(1)}, f32[2,40,160]{2,1,0:T(8,128)S(1)}, u32[]{:S(2)}, u32[]{:S(2)}) %collective-permute-start.32) | collective-permute-done | bytes 51232 | tf_op jit(solution)/shard_map/ppermute | solution.py:197
  182.3 7.4 %collective-permute-done.33 = f32[2,40,160]{2,1,0:T(8,128)S(1)} collective-permute-done((f32[2,40,160]{2,1,0:T(8,128)S(1)}, f32[2,40,160]{2,1,0:T(8,128)S(1)}, u32[]{:S(2)}, u32[]{:S(2)}) %collective-permute-start.33) | collective-permute-done | bytes 51232 | tf_op jit(solution)/shard_map/ppermute | solution.py:197
  (97 shorter events, 34.4 us)
Async XLA Ops:
  3.2 9.3 %collective-permute-start.3 = (bf16[8,1,160,128]{3,2,1,0:T(8,128)(2,1)S(1)}, bf16[8,1,160,128]{3,2,1,0:T(8,128)(2,1)S(1)}, u32[]{:S(2)}, u32[]{:S(2)}) collective-permute-start(bf16[8,1,160,128]{3,2,1,0:T(8,128)(2,1)S(1)} %get-tuple-element.27), channel_id=1, source_target_pairs={{0,3},{1,0},{2,1},{3,2},{4,7},{5,4},{6,5},{7,6},{8,11},{9,8},{10,9... | collective-permute-start | bytes 983048 | tf_op jit(solution)/shard_map/ppermute | solution.py:155
  5.1 9.8 %collective-permute-start.2 = (bf16[8,1,160,128]{3,2,1,0:T(8,128)(2,1)S(1)}, bf16[8,1,160,128]{3,2,1,0:T(8,128)(2,1)S(1)}, u32[]{:S(2)}, u32[]{:S(2)}) collective-permute-start(bf16[8,1,160,128]{3,2,1,0:T(8,128)(2,1)S(1)} %get-tuple-element.28), channel_id=1, source_target_pairs={{0,1},{1,2},{2,3},{3,0},{4,5},{5,6},{6,7},{7,4},{8,9},{9,10},{10,1... | collective-permute-start | bytes 983048 | tf_op jit(solution)/shard_map/ppermute | solution.py:155
  5.8 17.7 %collective-permute-start.1 = (bf16[1,4,160,128]{3,2,1,0:T(8,128)(2,1)}, bf16[1,4,160,128]{3,2,1,0:T(8,128)(2,1)}, u32[]{:S(2)}, u32[]{:S(2)}) collective-permute-start(bf16[1,4,160,128]{3,2,1,0:T(8,128)(2,1)} %get-tuple-element.29), channel_id=1, source_target_pairs={{0,252},{4,0},{8,4},{12,8},{16,12},{20,16},{24,20},{28,24},{32,28}... | collective-permute-start | bytes 491528 | tf_op jit(solution)/shard_map/ppermute | solution.py:155
  9.4 14.1 %collective-permute-start = (bf16[1,4,160,128]{3,2,1,0:T(8,128)(2,1)}, bf16[1,4,160,128]{3,2,1,0:T(8,128)(2,1)}, u32[]{:S(2)}, u32[]{:S(2)}) collective-permute-start(bf16[1,4,160,128]{3,2,1,0:T(8,128)(2,1)} %get-tuple-element.30), channel_id=1, source_target_pairs={{0,4},{4,8},{8,12},{12,16},{16,20},{20,24},{24,28},{28,32},{32,36}... | collective-permute-start | bytes 491528 | tf_op jit(solution)/shard_map/ppermute | solution.py:155
  16.2 9.0 %collective-permute-start.4 = (bf16[1,2,160,128]{3,2,1,0:T(8,128)(2,1)}, bf16[1,2,160,128]{3,2,1,0:T(8,128)(2,1)S(1)}, u32[]{:S(2)}, u32[]{:S(2)}) collective-permute-start(bf16[1,2,160,128]{3,2,1,0:T(8,128)(2,1)} %pad_maximum_fusion), channel_id=1, source_target_pairs={{0,4},{4,8},{8,12},{12,16},{16,20},{20,24},{24,28},{28,32},{32,36}... | collective-permute-start | bytes 245768 | tf_op jit(solution)/shard_map/ppermute | solution.py:155
  18.4 7.3 %collective-permute-start.5 = (bf16[1,2,160,128]{3,2,1,0:T(8,128)(2,1)}, bf16[1,2,160,128]{3,2,1,0:T(8,128)(2,1)}, u32[]{:S(2)}, u32[]{:S(2)}) collective-permute-start(bf16[1,2,160,128]{3,2,1,0:T(8,128)(2,1)} %pad_maximum_fusion.1), channel_id=1, source_target_pairs={{0,252},{4,0},{8,4},{12,8},{16,12},{20,16},{24,20},{28,24},{32,28}... | collective-permute-start | bytes 245768 | tf_op jit(solution)/shard_map/ppermute | solution.py:155
  39.6 10.6 %collective-permute-start.9 = (bf16[8,1,160,128]{3,2,1,0:T(8,128)(2,1)S(1)}, bf16[8,1,160,128]{3,2,1,0:T(8,128)(2,1)S(1)}, u32[]{:S(2)}, u32[]{:S(2)}) collective-permute-start(bf16[8,1,160,128]{3,2,1,0:T(8,128)(2,1)S(1)} %get-tuple-element.23), channel_id=1, source_target_pairs={{0,3},{1,0},{2,1},{3,2},{4,7},{5,4},{6,5},{7,6},{8,11},{9,8},{10,9... | collective-permute-start | bytes 983048 | tf_op jit(solution)/shard_map/ppermute | solution.py:155
  42.2 9.0 %collective-permute-start.8 = (bf16[8,1,160,128]{3,2,1,0:T(8,128)(2,1)S(1)}, bf16[8,1,160,128]{3,2,1,0:T(8,128)(2,1)S(1)}, u32[]{:S(2)}, u32[]{:S(2)}) collective-permute-start(bf16[8,1,160,128]{3,2,1,0:T(8,128)(2,1)S(1)} %get-tuple-element.24), channel_id=1, source_target_pairs={{0,1},{1,2},{2,3},{3,0},{4,5},{5,6},{6,7},{7,4},{8,9},{9,10},{10,1... | collective-permute-start | bytes 983048 | tf_op jit(solution)/shard_map/ppermute | solution.py:155
  42.2 17.0 %collective-permute-start.7 = (bf16[1,4,160,128]{3,2,1,0:T(8,128)(2,1)S(1)}, bf16[1,4,160,128]{3,2,1,0:T(8,128)(2,1)S(1)}, u32[]{:S(2)}, u32[]{:S(2)}) collective-permute-start(bf16[1,4,160,128]{3,2,1,0:T(8,128)(2,1)S(1)} %get-tuple-element.25), channel_id=1, source_target_pairs={{0,252},{4,0},{8,4},{12,8},{16,12},{20,16},{24,20},{28,24},{32,28}... | collective-permute-start | bytes 491528 | tf_op jit(solution)/shard_map/ppermute | solution.py:155
  47.5 11.7 %collective-permute-start.6 = (bf16[1,4,160,128]{3,2,1,0:T(8,128)(2,1)S(1)}, bf16[1,4,160,128]{3,2,1,0:T(8,128)(2,1)S(1)}, u32[]{:S(2)}, u32[]{:S(2)}) collective-permute-start(bf16[1,4,160,128]{3,2,1,0:T(8,128)(2,1)S(1)} %get-tuple-element.26), channel_id=1, source_target_pairs={{0,4},{4,8},{8,12},{12,16},{16,20},{20,24},{24,28},{28,32},{32,36}... | collective-permute-start | bytes 491528 | tf_op jit(solution)/shard_map/ppermute | solution.py:155
  51.2 10.4 %collective-permute-start.10 = (bf16[1,2,160,128]{3,2,1,0:T(8,128)(2,1)S(1)}, bf16[1,2,160,128]{3,2,1,0:T(8,128)(2,1)S(1)}, u32[]{:S(2)}, u32[]{:S(2)}) collective-permute-start(bf16[1,2,160,128]{3,2,1,0:T(8,128)(2,1)S(1)} %pad_maximum_fusion.2), channel_id=1, source_target_pairs={{0,4},{4,8},{8,12},{12,16},{16,20},{20,24},{24,28},{28,32},{32,36}... | collective-permute-start | bytes 245768 | tf_op jit(solution)/shard_map/ppermute | solution.py:155
  52.4 9.2 %collective-permute-start.11 = (bf16[1,2,160,128]{3,2,1,0:T(8,128)(2,1)S(1)}, bf16[1,2,160,128]{3,2,1,0:T(8,128)(2,1)S(1)}, u32[]{:S(2)}, u32[]{:S(2)}) collective-permute-start(bf16[1,2,160,128]{3,2,1,0:T(8,128)(2,1)S(1)} %pad_maximum_fusion.3), channel_id=1, source_target_pairs={{0,252},{4,0},{8,4},{12,8},{16,12},{20,16},{24,20},{28,24},{32,28}... | collective-permute-start | bytes 245768 | tf_op jit(solution)/shard_map/ppermute | solution.py:155
  69.4 10.4 %collective-permute-start.15 = (bf16[8,1,160,128]{3,2,1,0:T(8,128)(2,1)S(1)}, bf16[8,1,160,128]{3,2,1,0:T(8,128)(2,1)S(1)}, u32[]{:S(2)}, u32[]{:S(2)}) collective-permute-start(bf16[8,1,160,128]{3,2,1,0:T(8,128)(2,1)S(1)} %get-tuple-element.19), channel_id=1, source_target_pairs={{0,3},{1,0},{2,1},{3,2},{4,7},{5,4},{6,5},{7,6},{8,11},{9,8},{10,9... | collective-permute-start | bytes 983048 | tf_op jit(solution)/shard_map/ppermute | solution.py:155
  72.2 9.4 %collective-permute-start.14 = (bf16[8,1,160,128]{3,2,1,0:T(8,128)(2,1)S(1)}, bf16[8,1,160,128]{3,2,1,0:T(8,128)(2,1)S(1)}, u32[]{:S(2)}, u32[]{:S(2)}) collective-permute-start(bf16[8,1,160,128]{3,2,1,0:T(8,128)(2,1)S(1)} %get-tuple-element.20), channel_id=1, source_target_pairs={{0,1},{1,2},{2,3},{3,0},{4,5},{5,6},{6,7},{7,4},{8,9},{9,10},{10,1... | collective-permute-start | bytes 983048 | tf_op jit(solution)/shard_map/ppermute | solution.py:155
  72.2 14.1 %collective-permute-start.13 = (bf16[1,4,160,128]{3,2,1,0:T(8,128)(2,1)S(1)}, bf16[1,4,160,128]{3,2,1,0:T(8,128)(2,1)S(1)}, u32[]{:S(2)}, u32[]{:S(2)}) collective-permute-start(bf16[1,4,160,128]{3,2,1,0:T(8,128)(2,1)S(1)} %get-tuple-element.21), channel_id=1, source_target_pairs={{0,252},{4,0},{8,4},{12,8},{16,12},{20,16},{24,20},{28,24},{32,28}... | collective-permute-start | bytes 491528 | tf_op jit(solution)/shard_map/ppermute | solution.py:155
  76.5 9.8 %collective-permute-start.12 = (bf16[1,4,160,128]{3,2,1,0:T(8,128)(2,1)S(1)}, bf16[1,4,160,128]{3,2,1,0:T(8,128)(2,1)S(1)}, u32[]{:S(2)}, u32[]{:S(2)}) collective-permute-start(bf16[1,4,160,128]{3,2,1,0:T(8,128)(2,1)S(1)} %get-tuple-element.22), channel_id=1, source_target_pairs={{0,4},{4,8},{8,12},{12,16},{16,20},{20,24},{24,28},{28,32},{32,36}... | collective-permute-start | bytes 491528 | tf_op jit(solution)/shard_map/ppermute | solution.py:155
  81.6 7.0 %collective-permute-start.16 = (bf16[1,2,160,128]{3,2,1,0:T(8,128)(2,1)S(1)}, bf16[1,2,160,128]{3,2,1,0:T(8,128)(2,1)S(1)}, u32[]{:S(2)}, u32[]{:S(2)}) collective-permute-start(bf16[1,2,160,128]{3,2,1,0:T(8,128)(2,1)S(1)} %pad_maximum_fusion.4), channel_id=1, source_target_pairs={{0,4},{4,8},{8,12},{12,16},{16,20},{20,24},{24,28},{28,32},{32,36}... | collective-permute-start | bytes 245768 | tf_op jit(solution)/shard_map/ppermute | solution.py:155
  100.9 8.2 %collective-permute-start.21 = (bf16[8,1,160,128]{3,2,1,0:T(8,128)(2,1)S(1)}, bf16[8,1,160,128]{3,2,1,0:T(8,128)(2,1)S(1)}, u32[]{:S(2)}, u32[]{:S(2)}) collective-permute-start(bf16[8,1,160,128]{3,2,1,0:T(8,128)(2,1)S(1)} %get-tuple-element.15), channel_id=1, source_target_pairs={{0,3},{1,0},{2,1},{3,2},{4,7},{5,4},{6,5},{7,6},{8,11},{9,8},{10,9... | collective-permute-start | bytes 983048 | tf_op jit(solution)/shard_map/ppermute | solution.py:155
  101.0 12.5 %collective-permute-start.20 = (bf16[8,1,160,128]{3,2,1,0:T(8,128)(2,1)S(1)}, bf16[8,1,160,128]{3,2,1,0:T(8,128)(2,1)S(1)}, u32[]{:S(2)}, u32[]{:S(2)}) collective-permute-start(bf16[8,1,160,128]{3,2,1,0:T(8,128)(2,1)S(1)} %get-tuple-element.16), channel_id=1, source_target_pairs={{0,1},{1,2},{2,3},{3,0},{4,5},{5,6},{6,7},{7,4},{8,9},{9,10},{10,1... | collective-permute-start | bytes 983048 | tf_op jit(solution)/shard_map/ppermute | solution.py:155
  101.5 17.5 %collective-permute-start.19 = (bf16[1,4,160,128]{3,2,1,0:T(8,128)(2,1)S(1)}, bf16[1,4,160,128]{3,2,1,0:T(8,128)(2,1)S(1)}, u32[]{:S(2)}, u32[]{:S(2)}) collective-permute-start(bf16[1,4,160,128]{3,2,1,0:T(8,128)(2,1)S(1)} %get-tuple-element.17), channel_id=1, source_target_pairs={{0,252},{4,0},{8,4},{12,8},{16,12},{20,16},{24,20},{28,24},{32,28}... | collective-permute-start | bytes 491528 | tf_op jit(solution)/shard_map/ppermute | solution.py:155
  105.4 13.6 %collective-permute-start.18 = (bf16[1,4,160,128]{3,2,1,0:T(8,128)(2,1)S(1)}, bf16[1,4,160,128]{3,2,1,0:T(8,128)(2,1)S(1)}, u32[]{:S(2)}, u32[]{:S(2)}) collective-permute-start(bf16[1,4,160,128]{3,2,1,0:T(8,128)(2,1)S(1)} %get-tuple-element.18), channel_id=1, source_target_pairs={{0,4},{4,8},{8,12},{12,16},{16,20},{20,24},{24,28},{28,32},{32,36}... | collective-permute-start | bytes 491528 | tf_op jit(solution)/shard_map/ppermute | solution.py:155
  113.5 7.8 %collective-permute-start.22 = (bf16[1,2,160,128]{3,2,1,0:T(8,128)(2,1)S(1)}, bf16[1,2,160,128]{3,2,1,0:T(8,128)(2,1)S(1)}, u32[]{:S(2)}, u32[]{:S(2)}) collective-permute-start(bf16[1,2,160,128]{3,2,1,0:T(8,128)(2,1)S(1)} %pad_maximum_fusion.6), channel_id=1, source_target_pairs={{0,4},{4,8},{8,12},{12,16},{16,20},{20,24},{24,28},{28,32},{32,36}... | collective-permute-start | bytes 245768 | tf_op jit(solution)/shard_map/ppermute | solution.py:155
  132.8 5.6 %collective-permute-start.24 = (f32[2,40,160]{2,1,0:T(8,128)S(1)}, f32[2,40,160]{2,1,0:T(8,128)S(1)}, u32[]{:S(2)}, u32[]{:S(2)}) collective-permute-start(f32[2,40,160]{2,1,0:T(8,128)S(1)} %get-tuple-element.12), channel_id=1, source_target_pairs={{0,1},{1,2},{2,3},{3,0},{4,5},{5,6},{6,7},{7,4},{8,9},{9,10},{10,1... | collective-permute-start | bytes 153608 | tf_op jit(solution)/shard_map/ppermute | solution.py:155
  132.8 6.6 %collective-permute-start.25 = (f32[2,40,160]{2,1,0:T(8,128)S(1)}, f32[2,40,160]{2,1,0:T(8,128)S(1)}, u32[]{:S(2)}, u32[]{:S(2)}) collective-permute-start(f32[2,40,160]{2,1,0:T(8,128)S(1)} %get-tuple-element.13), channel_id=1, source_target_pairs={{0,2},{1,3},{2,0},{3,1},{4,6},{5,7},{6,4},{7,5},{8,10},{9,11},{10,... | collective-permute-start | bytes 153608 | tf_op jit(solution)/shard_map/ppermute | solution.py:155
  134.6 4.9 %collective-permute-start.26 = (f32[2,40,160]{2,1,0:T(8,128)S(1)}, f32[2,40,160]{2,1,0:T(8,128)S(1)}, u32[]{:S(2)}, u32[]{:S(2)}) collective-permute-start(f32[2,40,160]{2,1,0:T(8,128)S(1)} %get-tuple-element.14), channel_id=1, source_target_pairs={{0,3},{1,0},{2,1},{3,2},{4,7},{5,4},{6,5},{7,6},{8,11},{9,8},{10,9... | collective-permute-start | bytes 153608 | tf_op jit(solution)/shard_map/ppermute | solution.py:155
  139.6 18.1 %collective-permute-start.29 = (f32[2,40,160]{2,1,0:T(8,128)S(1)}, f32[2,40,160]{2,1,0:T(8,128)S(1)}, u32[]{:S(2)}, u32[]{:S(2)}) collective-permute-start(f32[2,40,160]{2,1,0:T(8,128)S(1)} %add_add_fusion.1), channel_id=1, source_target_pairs={{0,12},{4,0},{8,4},{12,8},{1,13},{5,1},{9,5},{13,9},{2,14},{6,2},{... | collective-permute-start | bytes 153608 | tf_op jit(solution)/shard_map/ppermute | solution.py:197
  153.7 6.4 %collective-permute-start.28 = (f32[2,40,160]{2,1,0:T(8,128)S(1)}, f32[2,40,160]{2,1,0:T(8,128)S(1)}, u32[]{:S(2)}, u32[]{:S(2)}) collective-permute-start(f32[2,40,160]{2,1,0:T(8,128)S(1)} %add_add_fusion.1), channel_id=1, source_target_pairs={{0,8},{4,12},{8,0},{12,4},{1,9},{5,13},{9,1},{13,5},{2,10},{6,14},... | collective-permute-start | bytes 153608 | tf_op jit(solution)/shard_map/ppermute | solution.py:197
  153.7 7.9 %collective-permute-start.27 = (f32[2,40,160]{2,1,0:T(8,128)S(1)}, f32[2,40,160]{2,1,0:T(8,128)S(1)}, u32[]{:S(2)}, u32[]{:S(2)}) collective-permute-start(f32[2,40,160]{2,1,0:T(8,128)S(1)} %add_add_fusion.1), channel_id=1, source_target_pairs={{0,4},{4,8},{8,12},{12,0},{1,5},{5,9},{9,13},{13,1},{2,6},{6,10},{... | collective-permute-start | bytes 153608 | tf_op jit(solution)/shard_map/ppermute | solution.py:197
  161.6 4.6 %collective-permute-start.30 = (f32[2,40,160]{2,1,0:T(8,128)S(1)}, f32[2,40,160]{2,1,0:T(8,128)S(1)}, u32[]{:S(2)}, u32[]{:S(2)}) collective-permute-start(f32[2,40,160]{2,1,0:T(8,128)S(1)} %add_add_fusion), channel_id=1, source_target_pairs={{0,16},{16,0},{1,17},{17,1},{2,18},{18,2},{3,19},{19,3},{4,20},{20... | collective-permute-start | bytes 153608 | tf_op jit(solution)/shard_map/ppermute | solution.py:197
  166.3 4.5 %collective-permute-start.31 = (f32[2,40,160]{2,1,0:T(8,128)S(1)}, f32[2,40,160]{2,1,0:T(8,128)S(1)}, u32[]{:S(2)}, u32[]{:S(2)}) collective-permute-start(f32[2,40,160]{2,1,0:T(8,128)S(1)} %add.60), channel_id=1, source_target_pairs={{0,32},{32,0},{64,96},{96,64},{128,160},{160,128},{192,224},{224,1... | collective-permute-start | bytes 153608 | tf_op jit(solution)/shard_map/ppermute | solution.py:197
  170.8 11.3 %collective-permute-start.32 = (f32[2,40,160]{2,1,0:T(8,128)S(1)}, f32[2,40,160]{2,1,0:T(8,128)S(1)}, u32[]{:S(2)}, u32[]{:S(2)}) collective-permute-start(f32[2,40,160]{2,1,0:T(8,128)S(1)} %add.61), channel_id=1, source_target_pairs={{0,64},{32,96},{64,0},{96,32},{128,192},{160,224},{192,128},{224,1... | collective-permute-start | bytes 153608 | tf_op jit(solution)/shard_map/ppermute | solution.py:197
  182.2 7.5 %collective-permute-start.33 = (f32[2,40,160]{2,1,0:T(8,128)S(1)}, f32[2,40,160]{2,1,0:T(8,128)S(1)}, u32[]{:S(2)}, u32[]{:S(2)}) collective-permute-start(f32[2,40,160]{2,1,0:T(8,128)S(1)} %add.62), channel_id=1, source_target_pairs={{0,224},{32,192},{64,160},{96,128},{128,96},{160,64},{192,32},{224... | collective-permute-start | bytes 153608 | tf_op jit(solution)/shard_map/ppermute | solution.py:197
  (12 other events, 128.7 us)

commit v2 on v0

v2 whole, which is shorter than its diff:
```python
import functools

import jax
import jax.numpy as jnp
from jax import lax
from jax.experimental import pallas as pl
from jax.experimental.pallas import tpu as pltpu
from jax.sharding import Mesh, PartitionSpec as P


CENTER = 0.25
INV_HALF = 1.0 / 1.5
VMEM = pl.BlockSpec(memory_space=pltpu.VMEM)
SMEM = pl.BlockSpec(memory_space=pltpu.SMEM)
BF16, F32 = jnp.bfloat16, jnp.float32


def nt_dot(a, b):
    return lax.dot_general(a, b, (((1,), (1,)), ((), ())), preferred_element_type=F32)


def call(body, out_shape, args, in_specs=None, scratch=(), flops=0):
    return pl.pallas_call(
        body,
        out_shape=out_shape,
        in_specs=in_specs or [VMEM] * len(args),
        out_specs=jax.tree.map(lambda _: VMEM, out_shape),
        scratch_shapes=scratch,
        compiler_params=pltpu.CompilerParams(vmem_limit_bytes=16 * 1024 * 1024),
        cost_estimate=pl.CostEstimate(flops=flops, bytes_accessed=8_000_000, transcendentals=0),
    )(*args)


def step_kernel(mode, dims, *refs):
    rows, cols, columns, basis, neighbours = dims
    wide = cols + 2
    refs = list(refs)
    index, count, v, low, high, left, right, corner_left, corner_right, selfs, near = refs[:11]
    del refs[:11]
    prev = refs.pop(0) if mode in ("second", "third") else None
    if mode == "image":
        band, gram = refs[:2]
        pieces, ext, acc = refs[2:6], refs[6], refs[7]
        acc[...] = jnp.zeros_like(acc)
    else:
        out, col_right, col_left, row_low, row_high, ext = refs
    lane = lax.broadcasted_iota(jnp.int32, (columns, basis), 1)
    last = (rows + 1) * wide
    for j in range(cols):
        ext[1 + j] = low[0, j]
        ext[last + 1 + j] = high[0, j]
    for t in range(2):
        ext[t * last] = corner_left[t, 0]
        ext[t * last + wide - 1] = corner_right[t, 0]

    def fill(r, carry):
        for j in range(cols):
            ext[(r + 1) * wide + 1 + j] = v[r, j]
        ext[(r + 1) * wide] = left[r, 0]
        ext[(r + 1) * wide + wide - 1] = right[r, 0]
        return carry

    lax.fori_loop(0, rows, fill, 0)

    def one_row(i, carry):
        made, held = [], []
        for j in range(cols):
            own = ext[(i + 1) * wide + j + 1]
            tiles = [ext[index[i, j * neighbours + k]] for k in range(neighbours)]
            total = jnp.dot(own, selfs[i, j], preferred_element_type=F32)
            for k in range(0, neighbours, 2):
                lhs = jnp.concatenate([tiles[k], tiles[k + 1]], axis=1)
                rhs = near[i, j, k : k + 2].reshape(2 * basis, basis)
                total = total + jnp.dot(lhs, rhs, preferred_element_type=F32)
            total = jnp.where(lane < count[i, j], total, 0.0)
            if mode != "image":
                total = (total - CENTER * own.astype(F32)) * INV_HALF
                if mode != "first":
                    total = 2.0 * total - prev[i, j].astype(F32)
            result = total.astype(BF16)
            if mode == "image":
                made.append(result)
                held.append(own)
                continue
            out[i, j] = result
            if j == 0:
                col_left[i, 0] = result
            if j == cols - 1:
                col_right[i, 0] = result
        if mode == "image":
            acc[...] += nt_dot(jnp.concatenate(held, axis=1), jnp.concatenate(made, axis=1))
        return carry

    lax.fori_loop(0, rows, one_row, 0)
    if mode != "image":
        for j in range(cols):
            row_low[0, j] = out[rows - 1, j]
            row_high[0, j] = out[0, j]
        return
    share = columns // 4
    for s in range(4):
        first = pl.multiple_of(lax.rem(band[0] + s, 4) * share, 8)
        pieces[s][0] = gram[pl.ds(first, share), :]
        pieces[s][1] = acc[pl.ds(first, share), :]


def start_kernel(x, count, out, col_right, col_left, row_low, row_high):
    rows, cols, columns, basis = x.shape
    lane = lax.broadcasted_iota(jnp.int32, (columns, basis), 1)

    def one(r, c):
        for j in range(cols):
            value = jnp.where(lane < count[r, j], x[r, j].astype(F32), 0.0).astype(BF16)
            out[r, j] = value
            if j == 0:
                col_left[r, 0] = value
            if j == cols - 1:
                col_right[r, 0] = value
        return c

    lax.fori_loop(0, rows, one, 0)
    for j in range(cols):
        row_low[0, j] = out[rows - 1, j]
        row_high[0, j] = out[0, j]


def relay_kernel(low, high, send_right, send_left):
    cols = low.shape[1]
    for t, halo in enumerate((low, high)):
        send_right[t, 0] = halo[0, cols - 1]
        send_left[t, 0] = halo[0, 0]


def gram_kernel(v, gram):
    rows, cols = v.shape[:2]
    gram[...] = jnp.zeros_like(gram)

    def one(r, c):
        wide_v = jnp.concatenate([v[r, j] for j in range(cols)], axis=1)
        gram[...] += nt_dot(wide_v, wide_v)
        return c

    lax.fori_loop(0, rows, one, 0)


def shifted(value, axes, count, step):
    return lax.ppermute(value, axes, [(p, (p + step) % count) for p in range(count)])


def on_device(elem, band, sizes, basis_counts, neighbour_codes, x_block, h_self, h_near):
    rows, cols, columns, basis = x_block.shape
    neighbours = neighbour_codes.shape[2]
    dims = (rows, cols, columns, basis, neighbours)
    wide = cols + 2
    n_elem, n_band = sizes
    row_iota = lax.broadcasted_iota(jnp.int32, (rows, cols, neighbours), 0)
    col_iota = lax.broadcasted_iota(jnp.int32, (rows, cols, neighbours), 1)
    index = (
        (row_iota + neighbour_codes // 3) * wide + col_iota + neighbour_codes % 3
    ).reshape(rows, cols * neighbours)
    band_at = lax.axis_index(band).astype(jnp.int32).reshape(1)
    shape = lambda *s: jax.ShapeDtypeStruct(s, BF16)
    block = [
        shape(rows, cols, columns, basis),
        shape(rows, 1, columns, basis),
        shape(rows, 1, columns, basis),
        shape(1, cols, columns, basis),
        shape(1, cols, columns, basis),
    ]
    square = jax.ShapeDtypeStruct((columns, columns), F32)
    per_element = 2 * columns * basis * basis * (neighbours + 1)

    current = call(start_kernel, block, [x_block, basis_counts], in_specs=[VMEM, SMEM])
    older, gram = None, None
    for mode in ("first", "second", "third", "image"):
        v, col_right, col_left, row_low, row_high = current
        left = shifted(col_right, band, n_band, 1)
        right = shifted(col_left, band, n_band, -1)
        low = shifted(row_low, elem, n_elem, 1)
        high = shifted(row_high, elem, n_elem, -1)
        relay = [shape(2, 1, columns, basis)] * 2
        send_right, send_left = call(relay_kernel, relay, [low, high])
        corner_left = shifted(send_right, band, n_band, 1)
        corner_right = shifted(send_left, band, n_band, -1)
        prev = [older] if mode in ("second", "third") else []
        args = [index, basis_counts, v, low, high, left, right, corner_left, corner_right]
        args += [h_self, h_near, *prev]
        specs = [SMEM, SMEM] + [VMEM] * (len(args) - 2)
        scratch = [pltpu.VMEM(((rows + 2) * wide, columns, basis), BF16)]
        if mode == "image":
            gram = call(gram_kernel, square, [v], flops=2 * 32 * columns * columns * basis)
            args += [band_at, gram]
            specs += [SMEM, VMEM]
            scratch.append(pltpu.VMEM((columns, columns), F32))
            out_shape = [jax.ShapeDtypeStruct((2, columns // 4, columns), F32)] * 4
        else:
            out_shape = block
        done = call(
            functools.partial(step_kernel, mode, dims),
            out_shape,
            args,
            in_specs=specs,
            scratch=scratch,
            flops=32 * per_element,
        )
        if mode == "image":
            filtered, pieces = v, done
        else:
            older, current = v, done

    total = pieces[0]
    for s in range(1, n_band):
        total = total + shifted(pieces[s], band, n_band, s)

    def fold(value, axis, maps):
        moved = [lax.ppermute(value, axis, pairs) for pairs in maps]
        return sum(moved, value)

    total = fold(total, "x", [[(p, (p + s) % 4) for p in range(4)] for s in (1, 2, 3)])
    total = fold(total, "yl", [[(p, 1 - p) for p in range(2)]])
    for pairs in ([(p, p ^ 1) for p in range(8)], [(p, p ^ 2) for p in range(8)], [(p, 7 - p) for p in range(8)]):
        total = fold(total, "z", [pairs])
    normalizer = jnp.float32(rows * cols * n_elem * n_band * basis / 3.0)
    total = total / normalizer
    return filtered, total[0], total[1]


def solution(mesh):
    split = Mesh(mesh.devices.reshape(8, 2, 4, 2, 2), ("z", "yl", "x", "yh", "core"))
    elem, band = ("z", "yl", "x"), ("yh", "core")
    in_specs = (P(elem, band),) + tuple(P(elem, band, *[None] * n) for n in (1, 2, 2, 3))
    out_specs = (P(elem, band, None, None), P(band, None), P(band, None))
    body = functools.partial(on_device, elem, band, (64, 4))
    return jax.shard_map(body, mesh=split, in_specs=in_specs, out_specs=out_specs, check_vma=False)
```

time: 457 us -> 151 us (0.33)
  the two profiles are of different devices: /device:TPU:1 before, /device:TPU:40 now
where the time goes in v2:
time: 151 us
  starting transfers between devices  68.9 us (46%)
  waiting for transfers between devices  45.8 us (30%)
  Pallas kernels  25.3 us (17%)
  local copies, waits for them, and re-layouts  9.88 us (7%)
    ppermute x27, starting transfers between devices, shifted(): lax.ppermute(value, axes, [(p, (p + step) % count) for p in range(count)])  47.8 us
    pallas_call x10, Pallas kernels, call(): pl.pallas_call(body, out_shape=out_shape, in_specs=in_specs or [VMEM] * l...  25.3 us
    ppermute x27, waiting for transfers between devices, shifted(): lax.ppermute(value, axes, [(p, (p + step) % count) for p in range(count)])  24.8 us
    ppermute x7, starting transfers between devices, fold(): moved = [lax.ppermute(value, axis, pairs) for pairs in maps]  21.1 us
    ppermute x7, waiting for transfers between devices, fold(): moved = [lax.ppermute(value, axis, pairs) for pairs in maps]  21 us
    unnamed x17, local copies, waits for them, and re-layouts  9.05 us
  transfers between devices with their start and end apart: 34, of which 16 were waited for; matrix products, arithmetic and copies ran while one was open for 0% of the time, Pallas kernels for 2%

profile of v2, /device:TPU:40, one launch (start us, length us, event | category | flops | bytes accessed | tf_op | source)
XLA Modules:
  0.0 150.9 jit_solution(14285624965671251243)
XLA Ops:
  6.0 2.6 %collective-permute-start.1 = (bf16[1,4,160,128]{3,2,1,0:T(8,128)(2,1)S(1)}, bf16[1,4,160,128]{3,2,1,0:T(8,128)(2,1)S(1)}, u32[]{:S(2)}, u32[]{:S(2)}) collective-permute-start(bf16[1,4,160,128]{3,2,1,0:T(8,128)(2,1)S(1)} %get-tuple-element.37), channel_id=1, source_target_pairs={{0,252},{4,0},{8,4},{12,8},{16,12},{20,16},{24,20},{28,24},{32,28}... | collective-permute-start | bytes 491528 | tf_op jit(solution)/shard_map/ppermute | solution.py:147
  8.6 3.2 %collective-permute-start.3 = (bf16[8,1,160,128]{3,2,1,0:T(8,128)(2,1)}, bf16[8,1,160,128]{3,2,1,0:T(8,128)(2,1)S(1)}, u32[]{:S(2)}, u32[]{:S(2)}) collective-permute-start(bf16[8,1,160,128]{3,2,1,0:T(8,128)(2,1)} %get-tuple-element.39), channel_id=1, source_target_pairs={{0,3},{1,0},{2,1},{3,2},{4,7},{5,4},{6,5},{7,6},{8,11},{9,8},{10,9... | collective-permute-start | bytes 983048 | tf_op jit(solution)/shard_map/ppermute | solution.py:147
  13.2 3.2 %collective-permute-start.5 = (bf16[2,1,160,128]{3,2,1,0:T(8,128)(2,1)}, bf16[2,1,160,128]{3,2,1,0:T(8,128)(2,1)S(1)}, u32[]{:S(2)}, u32[]{:S(2)}) collective-permute-start(bf16[2,1,160,128]{3,2,1,0:T(8,128)(2,1)} %get-tuple-element.41), channel_id=1, source_target_pairs={{0,3},{1,0},{2,1},{3,2},{4,7},{5,4},{6,5},{7,6},{8,11},{9,8},{10,9... | collective-permute-start | bytes 245768 | tf_op jit(solution)/shard_map/ppermute | solution.py:147
  16.7 5.0 %collective-permute-done.4.refs_7_ = bf16[2,1,160,128]{3,2,1,0:T(8,128)(2,1)S(1)} collective-permute-done((bf16[2,1,160,128]{3,2,1,0:T(8,128)(2,1)}, bf16[2,1,160,128]{3,2,1,0:T(8,128)(2,1)S(1)}, u32[]{:S(2)}, u32[]{:S(2)}) %collective-permute-start.4) | collective-permute-done | bytes 81952 | tf_op jit(solution)/shard_map/ppermute | solution.py:147
  21.8 2.8 %copy-done = bf16[8,4,6,128,128]{4,3,2,1,0:T(8,128)(2,1)S(1)} copy-done((bf16[8,4,6,128,128]{4,3,2,1,0:T(8,128)(2,1)S(1)}, bf16[8,4,6,128,128]{4,3,2,1,0:T(8,128)(2,1)}, u32[]{:S(2)}) %copy-start) | copy-done | bytes 6291480
  24.6 4.6 %shard_map.78 = (bf16[8,4,160,128]{3,2,1,0:T(8,128)(2,1)S(1)}, bf16[8,1,160,128]{3,2,1,0:T(8,128)(2,1)S(1)}, bf16[8,1,160,128]{3,2,1,0:T(8,128)(2,1)S(1)}, bf16[...) custom-call(s32[8,24]{1,0:T(8,128)S(1)} %reshape.12.refs_0_, s32[8,4]{1,0:T(8,128)S(1)} %copy.18.count.refs_1_, ...), custom_call_target="tpu_custom_call" | custom-call | flops 1174405120 | bytes 8000000 | tf_op jit(solution)/shard_map/pallas_call | solution.py:23
  32.5 4.1 %collective-permute-start.7 = (bf16[1,4,160,128]{3,2,1,0:T(8,128)(2,1)S(1)}, bf16[1,4,160,128]{3,2,1,0:T(8,128)(2,1)S(1)}, u32[]{:S(2)}, u32[]{:S(2)}) collective-permute-start(bf16[1,4,160,128]{3,2,1,0:T(8,128)(2,1)S(1)} %get-tuple-element.44), channel_id=1, source_target_pairs={{0,252},{4,0},{8,4},{12,8},{16,12},{20,16},{24,20},{28,24},{32,28}... | collective-permute-start | bytes 491528 | tf_op jit(solution)/shard_map/ppermute | solution.py:147
  36.7 4.6 %collective-permute-done.6.low.refs_3_ = bf16[1,4,160,128]{3,2,1,0:T(8,128)(2,1)S(1)} collective-permute-done((bf16[1,4,160,128]{3,2,1,0:T(8,128)(2,1)S(1)}, bf16[1,4,160,128]{3,2,1,0:T(8,128)(2,1)S(1)}, u32[]{:S(2)}, u32[]{:S(2)}) %collective-permute-start.6) | collective-permute-done | bytes 163872 | tf_op jit(solution)/shard_map/ppermute | solution.py:147
  41.4 3.2 %collective-permute-start.11 = (bf16[2,1,160,128]{3,2,1,0:T(8,128)(2,1)S(1)}, bf16[2,1,160,128]{3,2,1,0:T(8,128)(2,1)S(1)}, u32[]{:S(2)}, u32[]{:S(2)}) collective-permute-start(bf16[2,1,160,128]{3,2,1,0:T(8,128)(2,1)S(1)} %get-tuple-element.48), channel_id=1, source_target_pairs={{0,3},{1,0},{2,1},{3,2},{4,7},{5,4},{6,5},{7,6},{8,11},{9,8},{10,9... | collective-permute-start | bytes 245768 | tf_op jit(solution)/shard_map/ppermute | solution.py:147
  44.7 2.1 %collective-permute-done.10.refs_7_ = bf16[2,1,160,128]{3,2,1,0:T(8,128)(2,1)S(1)} collective-permute-done((bf16[2,1,160,128]{3,2,1,0:T(8,128)(2,1)S(1)}, bf16[2,1,160,128]{3,2,1,0:T(8,128)(2,1)S(1)}, u32[]{:S(2)}, u32[]{:S(2)}) %collective-permute-start.10) | collective-permute-done | bytes 81952 | tf_op jit(solution)/shard_map/ppermute | solution.py:147
  46.8 4.7 %shard_map.80 = (bf16[8,4,160,128]{3,2,1,0:T(8,128)(2,1)S(1)}, bf16[8,1,160,128]{3,2,1,0:T(8,128)(2,1)S(1)}, bf16[8,1,160,128]{3,2,1,0:T(8,128)(2,1)S(1)}, bf16[...) custom-call(s32[8,24]{1,0:T(8,128)S(1)} %reshape.12.refs_0_, s32[8,4]{1,0:T(8,128)S(1)} %copy.18.count.refs_1_, ...), custom_call_target="tpu_custom_call" | custom-call | flops 1174405120 | bytes 8000000 | tf_op jit(solution)/shard_map/pallas_call | solution.py:23
  54.9 4.1 %collective-permute-start.13 = (bf16[1,4,160,128]{3,2,1,0:T(8,128)(2,1)S(1)}, bf16[1,4,160,128]{3,2,1,0:T(8,128)(2,1)S(1)}, u32[]{:S(2)}, u32[]{:S(2)}) collective-permute-start(bf16[1,4,160,128]{3,2,1,0:T(8,128)(2,1)S(1)} %get-tuple-element.51), channel_id=1, source_target_pairs={{0,252},{4,0},{8,4},{12,8},{16,12},{20,16},{24,20},{28,24},{32,28}... | collective-permute-start | bytes 491528 | tf_op jit(solution)/shard_map/ppermute | solution.py:147
  59.0 3.8 %collective-permute-done.12.low.refs_3_ = bf16[1,4,160,128]{3,2,1,0:T(8,128)(2,1)S(1)} collective-permute-done((bf16[1,4,160,128]{3,2,1,0:T(8,128)(2,1)S(1)}, bf16[1,4,160,128]{3,2,1,0:T(8,128)(2,1)S(1)}, u32[]{:S(2)}, u32[]{:S(2)}) %collective-permute-start.12) | collective-permute-done | bytes 163872 | tf_op jit(solution)/shard_map/ppermute | solution.py:147
  62.9 3.2 %collective-permute-start.17 = (bf16[2,1,160,128]{3,2,1,0:T(8,128)(2,1)S(1)}, bf16[2,1,160,128]{3,2,1,0:T(8,128)(2,1)S(1)}, u32[]{:S(2)}, u32[]{:S(2)}) collective-permute-start(bf16[2,1,160,128]{3,2,1,0:T(8,128)(2,1)S(1)} %get-tuple-element.55), channel_id=1, source_target_pairs={{0,3},{1,0},{2,1},{3,2},{4,7},{5,4},{6,5},{7,6},{8,11},{9,8},{10,9... | collective-permute-start | bytes 245768 | tf_op jit(solution)/shard_map/ppermute | solution.py:147
  66.2 2.1 %collective-permute-done.16.refs_7_ = bf16[2,1,160,128]{3,2,1,0:T(8,128)(2,1)S(1)} collective-permute-done((bf16[2,1,160,128]{3,2,1,0:T(8,128)(2,1)S(1)}, bf16[2,1,160,128]{3,2,1,0:T(8,128)(2,1)S(1)}, u32[]{:S(2)}, u32[]{:S(2)}) %collective-permute-start.16) | collective-permute-done | bytes 81952 | tf_op jit(solution)/shard_map/ppermute | solution.py:147
  68.3 5.7 %shard_map.82 = (bf16[8,4,160,128]{3,2,1,0:T(8,128)(2,1)}, bf16[8,1,160,128]{3,2,1,0:T(8,128)(2,1)S(1)}, bf16[8,1,160,128]{3,2,1,0:T(8,128)(2,1)S(1)}, bf16[1,4,...) custom-call(s32[8,24]{1,0:T(8,128)S(1)} %reshape.12.refs_0_, s32[8,4]{1,0:T(8,128)S(1)} %copy.18.count.refs_1_, ...), custom_call_target="tpu_custom_call" | custom-call | flops 1174405120 | bytes 8000000 | tf_op jit(solution)/shard_map/pallas_call | solution.py:23
  77.3 2.1 %collective-permute-start.18 = (bf16[1,4,160,128]{3,2,1,0:T(8,128)(2,1)S(1)}, bf16[1,4,160,128]{3,2,1,0:T(8,128)(2,1)S(1)}, u32[]{:S(2)}, u32[]{:S(2)}) collective-permute-start(bf16[1,4,160,128]{3,2,1,0:T(8,128)(2,1)S(1)} %get-tuple-element.57), channel_id=1, source_target_pairs={{0,4},{4,8},{8,12},{12,16},{16,20},{20,24},{24,28},{28,32},{32,36}... | collective-permute-start | bytes 491528 | tf_op jit(solution)/shard_map/ppermute | solution.py:147
  79.3 2.1 %collective-permute-start.19 = (bf16[1,4,160,128]{3,2,1,0:T(8,128)(2,1)S(1)}, bf16[1,4,160,128]{3,2,1,0:T(8,128)(2,1)S(1)}, u32[]{:S(2)}, u32[]{:S(2)}) collective-permute-start(bf16[1,4,160,128]{3,2,1,0:T(8,128)(2,1)S(1)} %get-tuple-element.58), channel_id=1, source_target_pairs={{0,252},{4,0},{8,4},{12,8},{16,12},{20,16},{24,20},{28,24},{32,28}... | collective-permute-start | bytes 491528 | tf_op jit(solution)/shard_map/ppermute | solution.py:147
  81.4 3.4 %collective-permute-done.18.low.refs_3_ = bf16[1,4,160,128]{3,2,1,0:T(8,128)(2,1)S(1)} collective-permute-done((bf16[1,4,160,128]{3,2,1,0:T(8,128)(2,1)S(1)}, bf16[1,4,160,128]{3,2,1,0:T(8,128)(2,1)S(1)}, u32[]{:S(2)}, u32[]{:S(2)}) %collective-permute-start.18) | collective-permute-done | bytes 163872 | tf_op jit(solution)/shard_map/ppermute | solution.py:147
  84.9 3.2 %collective-permute-start.23 = (bf16[2,1,160,128]{3,2,1,0:T(8,128)(2,1)S(1)}, bf16[2,1,160,128]{3,2,1,0:T(8,128)(2,1)S(1)}, u32[]{:S(2)}, u32[]{:S(2)}) collective-permute-start(bf16[2,1,160,128]{3,2,1,0:T(8,128)(2,1)S(1)} %get-tuple-element.62), channel_id=1, source_target_pairs={{0,3},{1,0},{2,1},{3,2},{4,7},{5,4},{6,5},{7,6},{8,11},{9,8},{10,9... | collective-permute-start | bytes 245768 | tf_op jit(solution)/shard_map/ppermute | solution.py:147
  91.2 2.8 %copy-done.2 = bf16[8,4,6,128,128]{4,3,2,1,0:T(8,128)(2,1)S(1)} copy-done((bf16[8,4,6,128,128]{4,3,2,1,0:T(8,128)(2,1)S(1)}, bf16[8,4,6,128,128]{4,3,2,1,0:T(8,128)(2,1)}, u32[]{:S(2)}) %copy-start.2) | copy-done | bytes 6291480
  94.0 6.2 %shard_map.85 = (f32[2,40,160]{2,1,0:T(8,128)S(1)}, f32[2,40,160]{2,1,0:T(8,128)S(1)}, f32[2,40,160]{2,1,0:T(8,128)S(1)}, f32[2,40,160]{2,1,0:T(8,128)S(1)}) custom-call(s32[8,24]{1,0:T(8,128)S(1)} %reshape.12.refs_0_, s32[8,4]{1,0:T(8,128)S(1)} %copy.18.count.refs_1_, bf16[8,4,160,128]{3,2,1,0:T(8,128)(2,1)S(1)} %copy-done.5, ...), custom_call_target="tpu_custom_call" | custom-call | flops 1174405120 | bytes 8000000 | tf_op jit(solution)/shard_map/pallas_call | solution.py:23
  105.7 2.4 %collective-permute-done.25 = f32[2,40,160]{2,1,0:T(8,128)S(1)} collective-permute-done((f32[2,40,160]{2,1,0:T(8,128)S(1)}, f32[2,40,160]{2,1,0:T(8,128)S(1)}, u32[]{:S(2)}, u32[]{:S(2)}) %collective-permute-start.25) | collective-permute-done | bytes 51232 | tf_op jit(solution)/shard_map/ppermute | solution.py:147
  108.1 3.4 %collective-permute-start.27 = (f32[2,40,160]{2,1,0:T(8,128)S(1)}, f32[2,40,160]{2,1,0:T(8,128)S(1)}, u32[]{:S(2)}, u32[]{:S(2)}) collective-permute-start(f32[2,40,160]{2,1,0:T(8,128)S(1)} %add_add_fusion.1), channel_id=1, source_target_pairs={{0,4},{4,8},{8,12},{12,0},{1,5},{5,9},{9,13},{13,1},{2,6},{6,10},{... | collective-permute-start | bytes 153608 | tf_op jit(solution)/shard_map/ppermute | solution.py:216
  111.4 5.1 %collective-permute-start.28 = (f32[2,40,160]{2,1,0:T(8,128)S(1)}, f32[2,40,160]{2,1,0:T(8,128)S(1)}, u32[]{:S(2)}, u32[]{:S(2)}) collective-permute-start(f32[2,40,160]{2,1,0:T(8,128)S(1)} %add_add_fusion.1), channel_id=1, source_target_pairs={{0,8},{4,12},{8,0},{12,4},{1,9},{5,13},{9,1},{13,5},{2,10},{6,14},... | collective-permute-start | bytes 153608 | tf_op jit(solution)/shard_map/ppermute | solution.py:216
  117.7 3.5 %collective-permute-done.28 = f32[2,40,160]{2,1,0:T(8,128)S(1)} collective-permute-done((f32[2,40,160]{2,1,0:T(8,128)S(1)}, f32[2,40,160]{2,1,0:T(8,128)S(1)}, u32[]{:S(2)}, u32[]{:S(2)}) %collective-permute-start.28) | collective-permute-done | bytes 51232 | tf_op jit(solution)/shard_map/ppermute | solution.py:216
  121.8 4.4 %collective-permute-done.30 = f32[2,40,160]{2,1,0:T(8,128)S(1)} collective-permute-done((f32[2,40,160]{2,1,0:T(8,128)S(1)}, f32[2,40,160]{2,1,0:T(8,128)S(1)}, u32[]{:S(2)}, u32[]{:S(2)}) %collective-permute-start.30) | collective-permute-done | bytes 51232 | tf_op jit(solution)/shard_map/ppermute | solution.py:216
  126.2 4.0 %collective-permute-start.31 = (f32[2,40,160]{2,1,0:T(8,128)S(1)}, f32[2,40,160]{2,1,0:T(8,128)S(1)}, u32[]{:S(2)}, u32[]{:S(2)}) collective-permute-start(f32[2,40,160]{2,1,0:T(8,128)S(1)} %add.60), channel_id=1, source_target_pairs={{0,32},{32,0},{64,96},{96,64},{128,160},{160,128},{192,224},{224,1... | collective-permute-start | bytes 153608 | tf_op jit(solution)/shard_map/ppermute | solution.py:216
  130.3 2.4 %collective-permute-done.31 = f32[2,40,160]{2,1,0:T(8,128)S(1)} collective-permute-done((f32[2,40,160]{2,1,0:T(8,128)S(1)}, f32[2,40,160]{2,1,0:T(8,128)S(1)}, u32[]{:S(2)}, u32[]{:S(2)}) %collective-permute-start.31) | collective-permute-done | bytes 51232 | tf_op jit(solution)/shard_map/ppermute | solution.py:216
  132.7 7.5 %collective-permute-start.32 = (f32[2,40,160]{2,1,0:T(8,128)S(1)}, f32[2,40,160]{2,1,0:T(8,128)S(1)}, u32[]{:S(2)}, u32[]{:S(2)}) collective-permute-start(f32[2,40,160]{2,1,0:T(8,128)S(1)} %add.61), channel_id=1, source_target_pairs={{0,64},{32,96},{64,0},{96,32},{128,192},{160,224},{192,128},{224,1... | collective-permute-start | bytes 153608 | tf_op jit(solution)/shard_map/ppermute | solution.py:216
  140.3 2.4 %collective-permute-done.32 = f32[2,40,160]{2,1,0:T(8,128)S(1)} collective-permute-done((f32[2,40,160]{2,1,0:T(8,128)S(1)}, f32[2,40,160]{2,1,0:T(8,128)S(1)}, u32[]{:S(2)}, u32[]{:S(2)}) %collective-permute-start.32) | collective-permute-done | bytes 51232 | tf_op jit(solution)/shard_map/ppermute | solution.py:216
  143.6 6.6 %collective-permute-done.33 = f32[2,40,160]{2,1,0:T(8,128)S(1)} collective-permute-done((f32[2,40,160]{2,1,0:T(8,128)S(1)}, f32[2,40,160]{2,1,0:T(8,128)S(1)}, u32[]{:S(2)}, u32[]{:S(2)}) %collective-permute-start.33) | collective-permute-done | bytes 51232 | tf_op jit(solution)/shard_map/ppermute | solution.py:216
  (73 shorter events, 29.1 us)
Async XLA Ops:
  4.5 8.0 %collective-permute-start = (bf16[1,4,160,128]{3,2,1,0:T(8,128)(2,1)S(1)}, bf16[1,4,160,128]{3,2,1,0:T(8,128)(2,1)S(1)}, u32[]{:S(2)}, u32[]{:S(2)}) collective-permute-start(bf16[1,4,160,128]{3,2,1,0:T(8,128)(2,1)S(1)} %get-tuple-element.36), channel_id=1, source_target_pairs={{0,4},{4,8},{8,12},{12,16},{16,20},{20,24},{24,28},{28,32},{32,36}... | collective-permute-start | bytes 491528 | tf_op jit(solution)/shard_map/ppermute | solution.py:147
  6.0 6.6 %collective-permute-start.1 = (bf16[1,4,160,128]{3,2,1,0:T(8,128)(2,1)S(1)}, bf16[1,4,160,128]{3,2,1,0:T(8,128)(2,1)S(1)}, u32[]{:S(2)}, u32[]{:S(2)}) collective-permute-start(bf16[1,4,160,128]{3,2,1,0:T(8,128)(2,1)S(1)} %get-tuple-element.37), channel_id=1, source_target_pairs={{0,252},{4,0},{8,4},{12,8},{16,12},{20,16},{24,20},{28,24},{32,28}... | collective-permute-start | bytes 491528 | tf_op jit(solution)/shard_map/ppermute | solution.py:147
  8.6 13.1 %collective-permute-start.2 = (bf16[8,1,160,128]{3,2,1,0:T(8,128)(2,1)}, bf16[8,1,160,128]{3,2,1,0:T(8,128)(2,1)S(1)}, u32[]{:S(2)}, u32[]{:S(2)}) collective-permute-start(bf16[8,1,160,128]{3,2,1,0:T(8,128)(2,1)} %get-tuple-element.38), channel_id=1, source_target_pairs={{0,1},{1,2},{2,3},{3,0},{4,5},{5,6},{6,7},{7,4},{8,9},{9,10},{10,1... | collective-permute-start | bytes 983048 | tf_op jit(solution)/shard_map/ppermute | solution.py:147
  8.6 13.1 %collective-permute-start.3 = (bf16[8,1,160,128]{3,2,1,0:T(8,128)(2,1)}, bf16[8,1,160,128]{3,2,1,0:T(8,128)(2,1)S(1)}, u32[]{:S(2)}, u32[]{:S(2)}) collective-permute-start(bf16[8,1,160,128]{3,2,1,0:T(8,128)(2,1)} %get-tuple-element.39), channel_id=1, source_target_pairs={{0,3},{1,0},{2,1},{3,2},{4,7},{5,4},{6,5},{7,6},{8,11},{9,8},{10,9... | collective-permute-start | bytes 983048 | tf_op jit(solution)/shard_map/ppermute | solution.py:147
  13.2 8.5 %collective-permute-start.4 = (bf16[2,1,160,128]{3,2,1,0:T(8,128)(2,1)}, bf16[2,1,160,128]{3,2,1,0:T(8,128)(2,1)S(1)}, u32[]{:S(2)}, u32[]{:S(2)}) collective-permute-start(bf16[2,1,160,128]{3,2,1,0:T(8,128)(2,1)} %get-tuple-element.40), channel_id=1, source_target_pairs={{0,1},{1,2},{2,3},{3,0},{4,5},{5,6},{6,7},{7,4},{8,9},{9,10},{10,1... | collective-permute-start | bytes 245768 | tf_op jit(solution)/shard_map/ppermute | solution.py:147
  13.2 8.5 %collective-permute-start.5 = (bf16[2,1,160,128]{3,2,1,0:T(8,128)(2,1)}, bf16[2,1,160,128]{3,2,1,0:T(8,128)(2,1)S(1)}, u32[]{:S(2)}, u32[]{:S(2)}) collective-permute-start(bf16[2,1,160,128]{3,2,1,0:T(8,128)(2,1)} %get-tuple-element.41), channel_id=1, source_target_pairs={{0,3},{1,0},{2,1},{3,2},{4,7},{5,4},{6,5},{7,6},{8,11},{9,8},{10,9... | collective-permute-start | bytes 245768 | tf_op jit(solution)/shard_map/ppermute | solution.py:147
  29.2 17.6 %collective-permute-start.8 = (bf16[8,1,160,128]{3,2,1,0:T(8,128)(2,1)S(1)}, bf16[8,1,160,128]{3,2,1,0:T(8,128)(2,1)S(1)}, u32[]{:S(2)}, u32[]{:S(2)}) collective-permute-start(bf16[8,1,160,128]{3,2,1,0:T(8,128)(2,1)S(1)} %get-tuple-element.45), channel_id=1, source_target_pairs={{0,1},{1,2},{2,3},{3,0},{4,5},{5,6},{6,7},{7,4},{8,9},{9,10},{10,1... | collective-permute-start | bytes 983048 | tf_op jit(solution)/shard_map/ppermute | solution.py:147
  30.6 16.2 %collective-permute-start.9 = (bf16[8,1,160,128]{3,2,1,0:T(8,128)(2,1)S(1)}, bf16[8,1,160,128]{3,2,1,0:T(8,128)(2,1)S(1)}, u32[]{:S(2)}, u32[]{:S(2)}) collective-permute-start(bf16[8,1,160,128]{3,2,1,0:T(8,128)(2,1)S(1)} %get-tuple-element.46), channel_id=1, source_target_pairs={{0,3},{1,0},{2,1},{3,2},{4,7},{5,4},{6,5},{7,6},{8,11},{9,8},{10,9... | collective-permute-start | bytes 983048 | tf_op jit(solution)/shard_map/ppermute | solution.py:147
  32.5 8.8 %collective-permute-start.6 = (bf16[1,4,160,128]{3,2,1,0:T(8,128)(2,1)S(1)}, bf16[1,4,160,128]{3,2,1,0:T(8,128)(2,1)S(1)}, u32[]{:S(2)}, u32[]{:S(2)}) collective-permute-start(bf16[1,4,160,128]{3,2,1,0:T(8,128)(2,1)S(1)} %get-tuple-element.43), channel_id=1, source_target_pairs={{0,4},{4,8},{8,12},{12,16},{16,20},{20,24},{24,28},{28,32},{32,36}... | collective-permute-start | bytes 491528 | tf_op jit(solution)/shard_map/ppermute | solution.py:147
  32.5 8.8 %collective-permute-start.7 = (bf16[1,4,160,128]{3,2,1,0:T(8,128)(2,1)S(1)}, bf16[1,4,160,128]{3,2,1,0:T(8,128)(2,1)S(1)}, u32[]{:S(2)}, u32[]{:S(2)}) collective-permute-start(bf16[1,4,160,128]{3,2,1,0:T(8,128)(2,1)S(1)} %get-tuple-element.44), channel_id=1, source_target_pairs={{0,252},{4,0},{8,4},{12,8},{16,12},{20,16},{24,20},{28,24},{32,28}... | collective-permute-start | bytes 491528 | tf_op jit(solution)/shard_map/ppermute | solution.py:147
  41.3 5.4 %collective-permute-start.10 = (bf16[2,1,160,128]{3,2,1,0:T(8,128)(2,1)S(1)}, bf16[2,1,160,128]{3,2,1,0:T(8,128)(2,1)S(1)}, u32[]{:S(2)}, u32[]{:S(2)}) collective-permute-start(bf16[2,1,160,128]{3,2,1,0:T(8,128)(2,1)S(1)} %get-tuple-element.47), channel_id=1, source_target_pairs={{0,1},{1,2},{2,3},{3,0},{4,5},{5,6},{6,7},{7,4},{8,9},{9,10},{10,1... | collective-permute-start | bytes 245768 | tf_op jit(solution)/shard_map/ppermute | solution.py:147
  41.4 5.4 %collective-permute-start.11 = (bf16[2,1,160,128]{3,2,1,0:T(8,128)(2,1)S(1)}, bf16[2,1,160,128]{3,2,1,0:T(8,128)(2,1)S(1)}, u32[]{:S(2)}, u32[]{:S(2)}) collective-permute-start(bf16[2,1,160,128]{3,2,1,0:T(8,128)(2,1)S(1)} %get-tuple-element.48), channel_id=1, source_target_pairs={{0,3},{1,0},{2,1},{3,2},{4,7},{5,4},{6,5},{7,6},{8,11},{9,8},{10,9... | collective-permute-start | bytes 245768 | tf_op jit(solution)/shard_map/ppermute | solution.py:147
  51.5 16.8 %collective-permute-start.14 = (bf16[8,1,160,128]{3,2,1,0:T(8,128)(2,1)S(1)}, bf16[8,1,160,128]{3,2,1,0:T(8,128)(2,1)S(1)}, u32[]{:S(2)}, u32[]{:S(2)}) collective-permute-start(bf16[8,1,160,128]{3,2,1,0:T(8,128)(2,1)S(1)} %get-tuple-element.52), channel_id=1, source_target_pairs={{0,1},{1,2},{2,3},{3,0},{4,5},{5,6},{6,7},{7,4},{8,9},{9,10},{10,1... | collective-permute-start | bytes 983048 | tf_op jit(solution)/shard_map/ppermute | solution.py:147
  53.1 15.2 %collective-permute-start.15 = (bf16[8,1,160,128]{3,2,1,0:T(8,128)(2,1)S(1)}, bf16[8,1,160,128]{3,2,1,0:T(8,128)(2,1)S(1)}, u32[]{:S(2)}, u32[]{:S(2)}) collective-permute-start(bf16[8,1,160,128]{3,2,1,0:T(8,128)(2,1)S(1)} %get-tuple-element.53), channel_id=1, source_target_pairs={{0,3},{1,0},{2,1},{3,2},{4,7},{5,4},{6,5},{7,6},{8,11},{9,8},{10,9... | collective-permute-start | bytes 983048 | tf_op jit(solution)/shard_map/ppermute | solution.py:147
  54.9 7.9 %collective-permute-start.12 = (bf16[1,4,160,128]{3,2,1,0:T(8,128)(2,1)S(1)}, bf16[1,4,160,128]{3,2,1,0:T(8,128)(2,1)S(1)}, u32[]{:S(2)}, u32[]{:S(2)}) collective-permute-start(bf16[1,4,160,128]{3,2,1,0:T(8,128)(2,1)S(1)} %get-tuple-element.50), channel_id=1, source_target_pairs={{0,4},{4,8},{8,12},{12,16},{16,20},{20,24},{24,28},{28,32},{32,36}... | collective-permute-start | bytes 491528 | tf_op jit(solution)/shard_map/ppermute | solution.py:147
  54.9 7.9 %collective-permute-start.13 = (bf16[1,4,160,128]{3,2,1,0:T(8,128)(2,1)S(1)}, bf16[1,4,160,128]{3,2,1,0:T(8,128)(2,1)S(1)}, u32[]{:S(2)}, u32[]{:S(2)}) collective-permute-start(bf16[1,4,160,128]{3,2,1,0:T(8,128)(2,1)S(1)} %get-tuple-element.51), channel_id=1, source_target_pairs={{0,252},{4,0},{8,4},{12,8},{16,12},{20,16},{24,20},{28,24},{32,28}... | collective-permute-start | bytes 491528 | tf_op jit(solution)/shard_map/ppermute | solution.py:147
  62.9 5.4 %collective-permute-start.16 = (bf16[2,1,160,128]{3,2,1,0:T(8,128)(2,1)S(1)}, bf16[2,1,160,128]{3,2,1,0:T(8,128)(2,1)S(1)}, u32[]{:S(2)}, u32[]{:S(2)}) collective-permute-start(bf16[2,1,160,128]{3,2,1,0:T(8,128)(2,1)S(1)} %get-tuple-element.54), channel_id=1, source_target_pairs={{0,1},{1,2},{2,3},{3,0},{4,5},{5,6},{6,7},{7,4},{8,9},{9,10},{10,1... | collective-permute-start | bytes 245768 | tf_op jit(solution)/shard_map/ppermute | solution.py:147
  62.9 5.4 %collective-permute-start.17 = (bf16[2,1,160,128]{3,2,1,0:T(8,128)(2,1)S(1)}, bf16[2,1,160,128]{3,2,1,0:T(8,128)(2,1)S(1)}, u32[]{:S(2)}, u32[]{:S(2)}) collective-permute-start(bf16[2,1,160,128]{3,2,1,0:T(8,128)(2,1)S(1)} %get-tuple-element.55), channel_id=1, source_target_pairs={{0,3},{1,0},{2,1},{3,2},{4,7},{5,4},{6,5},{7,6},{8,11},{9,8},{10,9... | collective-permute-start | bytes 245768 | tf_op jit(solution)/shard_map/ppermute | solution.py:147
  74.0 17.2 %collective-permute-start.20 = (bf16[8,1,160,128]{3,2,1,0:T(8,128)(2,1)S(1)}, bf16[8,1,160,128]{3,2,1,0:T(8,128)(2,1)S(1)}, u32[]{:S(2)}, u32[]{:S(2)}) collective-permute-start(bf16[8,1,160,128]{3,2,1,0:T(8,128)(2,1)S(1)} %get-tuple-element.59), channel_id=1, source_target_pairs={{0,1},{1,2},{2,3},{3,0},{4,5},{5,6},{6,7},{7,4},{8,9},{9,10},{10,1... | collective-permute-start | bytes 983048 | tf_op jit(solution)/shard_map/ppermute | solution.py:147
  75.3 15.9 %collective-permute-start.21 = (bf16[8,1,160,128]{3,2,1,0:T(8,128)(2,1)S(1)}, bf16[8,1,160,128]{3,2,1,0:T(8,128)(2,1)S(1)}, u32[]{:S(2)}, u32[]{:S(2)}) collective-permute-start(bf16[8,1,160,128]{3,2,1,0:T(8,128)(2,1)S(1)} %get-tuple-element.60), channel_id=1, source_target_pairs={{0,3},{1,0},{2,1},{3,2},{4,7},{5,4},{6,5},{7,6},{8,11},{9,8},{10,9... | collective-permute-start | bytes 983048 | tf_op jit(solution)/shard_map/ppermute | solution.py:147
  77.3 7.5 %collective-permute-start.18 = (bf16[1,4,160,128]{3,2,1,0:T(8,128)(2,1)S(1)}, bf16[1,4,160,128]{3,2,1,0:T(8,128)(2,1)S(1)}, u32[]{:S(2)}, u32[]{:S(2)}) collective-permute-start(bf16[1,4,160,128]{3,2,1,0:T(8,128)(2,1)S(1)} %get-tuple-element.57), channel_id=1, source_target_pairs={{0,4},{4,8},{8,12},{12,16},{16,20},{20,24},{24,28},{28,32},{32,36}... | collective-permute-start | bytes 491528 | tf_op jit(solution)/shard_map/ppermute | solution.py:147
  79.3 5.5 %collective-permute-start.19 = (bf16[1,4,160,128]{3,2,1,0:T(8,128)(2,1)S(1)}, bf16[1,4,160,128]{3,2,1,0:T(8,128)(2,1)S(1)}, u32[]{:S(2)}, u32[]{:S(2)}) collective-permute-start(bf16[1,4,160,128]{3,2,1,0:T(8,128)(2,1)S(1)} %get-tuple-element.58), channel_id=1, source_target_pairs={{0,252},{4,0},{8,4},{12,8},{16,12},{20,16},{24,20},{28,24},{32,28}... | collective-permute-start | bytes 491528 | tf_op jit(solution)/shard_map/ppermute | solution.py:147
  84.8 6.4 %collective-permute-start.22 = (bf16[2,1,160,128]{3,2,1,0:T(8,128)(2,1)S(1)}, bf16[2,1,160,128]{3,2,1,0:T(8,128)(2,1)S(1)}, u32[]{:S(2)}, u32[]{:S(2)}) collective-permute-start(bf16[2,1,160,128]{3,2,1,0:T(8,128)(2,1)S(1)} %get-tuple-element.61), channel_id=1, source_target_pairs={{0,1},{1,2},{2,3},{3,0},{4,5},{5,6},{6,7},{7,4},{8,9},{9,10},{10,1... | collective-permute-start | bytes 245768 | tf_op jit(solution)/shard_map/ppermute | solution.py:147
  84.9 6.3 %collective-permute-start.23 = (bf16[2,1,160,128]{3,2,1,0:T(8,128)(2,1)S(1)}, bf16[2,1,160,128]{3,2,1,0:T(8,128)(2,1)S(1)}, u32[]{:S(2)}, u32[]{:S(2)}) collective-permute-start(bf16[2,1,160,128]{3,2,1,0:T(8,128)(2,1)S(1)} %get-tuple-element.62), channel_id=1, source_target_pairs={{0,3},{1,0},{2,1},{3,2},{4,7},{5,4},{6,5},{7,6},{8,11},{9,8},{10,9... | collective-permute-start | bytes 245768 | tf_op jit(solution)/shard_map/ppermute | solution.py:147
  100.2 5.4 %collective-permute-start.24 = (f32[2,40,160]{2,1,0:T(8,128)S(1)}, f32[2,40,160]{2,1,0:T(8,128)S(1)}, u32[]{:S(2)}, u32[]{:S(2)}) collective-permute-start(f32[2,40,160]{2,1,0:T(8,128)S(1)} %get-tuple-element.64), channel_id=1, source_target_pairs={{0,1},{1,2},{2,3},{3,0},{4,5},{5,6},{6,7},{7,4},{8,9},{9,10},{10,1... | collective-permute-start | bytes 153608 | tf_op jit(solution)/shard_map/ppermute | solution.py:147
  101.2 6.8 %collective-permute-start.25 = (f32[2,40,160]{2,1,0:T(8,128)S(1)}, f32[2,40,160]{2,1,0:T(8,128)S(1)}, u32[]{:S(2)}, u32[]{:S(2)}) collective-permute-start(f32[2,40,160]{2,1,0:T(8,128)S(1)} %get-tuple-element.65), channel_id=1, source_target_pairs={{0,2},{1,3},{2,0},{3,1},{4,6},{5,7},{6,4},{7,5},{8,10},{9,11},{10,... | collective-permute-start | bytes 153608 | tf_op jit(solution)/shard_map/ppermute | solution.py:147
  108.1 9.6 %collective-permute-start.27 = (f32[2,40,160]{2,1,0:T(8,128)S(1)}, f32[2,40,160]{2,1,0:T(8,128)S(1)}, u32[]{:S(2)}, u32[]{:S(2)}) collective-permute-start(f32[2,40,160]{2,1,0:T(8,128)S(1)} %add_add_fusion.1), channel_id=1, source_target_pairs={{0,4},{4,8},{8,12},{12,0},{1,5},{5,9},{9,13},{13,1},{2,6},{6,10},{... | collective-permute-start | bytes 153608 | tf_op jit(solution)/shard_map/ppermute | solution.py:216
  111.4 9.7 %collective-permute-start.28 = (f32[2,40,160]{2,1,0:T(8,128)S(1)}, f32[2,40,160]{2,1,0:T(8,128)S(1)}, u32[]{:S(2)}, u32[]{:S(2)}) collective-permute-start(f32[2,40,160]{2,1,0:T(8,128)S(1)} %add_add_fusion.1), channel_id=1, source_target_pairs={{0,8},{4,12},{8,0},{12,4},{1,9},{5,13},{9,1},{13,5},{2,10},{6,14},... | collective-permute-start | bytes 153608 | tf_op jit(solution)/shard_map/ppermute | solution.py:216
  116.5 5.2 %collective-permute-start.29 = (f32[2,40,160]{2,1,0:T(8,128)S(1)}, f32[2,40,160]{2,1,0:T(8,128)S(1)}, u32[]{:S(2)}, u32[]{:S(2)}) collective-permute-start(f32[2,40,160]{2,1,0:T(8,128)S(1)} %add_add_fusion.1), channel_id=1, source_target_pairs={{0,12},{4,0},{8,4},{12,8},{1,13},{5,1},{9,5},{13,9},{2,14},{6,2},{... | collective-permute-start | bytes 153608 | tf_op jit(solution)/shard_map/ppermute | solution.py:216
  126.2 6.5 %collective-permute-start.31 = (f32[2,40,160]{2,1,0:T(8,128)S(1)}, f32[2,40,160]{2,1,0:T(8,128)S(1)}, u32[]{:S(2)}, u32[]{:S(2)}) collective-permute-start(f32[2,40,160]{2,1,0:T(8,128)S(1)} %add.60), channel_id=1, source_target_pairs={{0,32},{32,0},{64,96},{96,64},{128,160},{160,128},{192,224},{224,1... | collective-permute-start | bytes 153608 | tf_op jit(solution)/shard_map/ppermute | solution.py:216
  132.7 10.0 %collective-permute-start.32 = (f32[2,40,160]{2,1,0:T(8,128)S(1)}, f32[2,40,160]{2,1,0:T(8,128)S(1)}, u32[]{:S(2)}, u32[]{:S(2)}) collective-permute-start(f32[2,40,160]{2,1,0:T(8,128)S(1)} %add.61), channel_id=1, source_target_pairs={{0,64},{32,96},{64,0},{96,32},{128,192},{160,224},{192,128},{224,1... | collective-permute-start | bytes 153608 | tf_op jit(solution)/shard_map/ppermute | solution.py:216
  142.7 7.5 %collective-permute-start.33 = (f32[2,40,160]{2,1,0:T(8,128)S(1)}, f32[2,40,160]{2,1,0:T(8,128)S(1)}, u32[]{:S(2)}, u32[]{:S(2)}) collective-permute-start(f32[2,40,160]{2,1,0:T(8,128)S(1)} %add.62), channel_id=1, source_target_pairs={{0,224},{32,192},{64,160},{96,128},{128,96},{160,64},{192,32},{224... | collective-permute-start | bytes 153608 | tf_op jit(solution)/shard_map/ppermute | solution.py:216
  (10 other events, 76.6 us)

commit v3 on v2

--- a/solution.py
+++ b/solution.py
@@ -11,6 +11,7 @@
 CENTER = 0.25
 INV_HALF = 1.0 / 1.5
 VMEM = pl.BlockSpec(memory_space=pltpu.VMEM)
+HBM = pl.BlockSpec(memory_space=pltpu.HBM)
 SMEM = pl.BlockSpec(memory_space=pltpu.SMEM)
 BF16, F32 = jnp.bfloat16, jnp.float32
 
@@ -19,12 +20,12 @@
     return lax.dot_general(a, b, (((1,), (1,)), ((), ())), preferred_element_type=F32)
 
 
-def call(body, out_shape, args, in_specs=None, scratch=(), flops=0):
+def call(body, out_shape, args, in_specs=None, out_specs=None, scratch=(), flops=0):
     return pl.pallas_call(
         body,
         out_shape=out_shape,
         in_specs=in_specs or [VMEM] * len(args),
-        out_specs=jax.tree.map(lambda _: VMEM, out_shape),
+        out_specs=out_specs or jax.tree.map(lambda _: VMEM, out_shape),
         scratch_shapes=scratch,
         compiler_params=pltpu.CompilerParams(vmem_limit_bytes=16 * 1024 * 1024),
         cost_estimate=pl.CostEstimate(flops=flops, bytes_accessed=8_000_000, transcendentals=0),
@@ -40,10 +41,17 @@
     prev = refs.pop(0) if mode in ("second", "third") else None
     if mode == "image":
         band, gram = refs[:2]
-        pieces, ext, acc = refs[2:6], refs[6], refs[7]
+        pieces = refs[2:6]
+        ext, acc, held_self, held_near, sems = refs[6:11]
+        self_hbm, near_hbm, selfs, near = selfs, near, held_self, held_near
+        for r in range(rows):
+            pltpu.make_async_copy(self_hbm.at[r], selfs.at[r], sems.at[0, r]).start()
+            pltpu.make_async_copy(near_hbm.at[r], near.at[r], sems.at[1, r]).start()
+    else:
+        out, col_right, col_left, row_low, row_high = refs[:5]
+        ext = refs[5]
+    if mode == "image":
         acc[...] = jnp.zeros_like(acc)
-    else:
-        out, col_right, col_left, row_low, row_high, ext = refs
     lane = lax.broadcasted_iota(jnp.int32, (columns, basis), 1)
     last = (rows + 1) * wide
     for j in range(cols):
@@ -64,6 +72,9 @@
 
     def one_row(i, carry):
         made, held = [], []
+        if mode == "image":
+            pltpu.make_async_copy(self_hbm.at[i], selfs.at[i], sems.at[0, i]).wait()
+            pltpu.make_async_copy(near_hbm.at[i], near.at[i], sems.at[1, i]).wait()
         for j in range(cols):
             own = ext[(i + 1) * wide + j + 1]
             tiles = [ext[index[i, j * neighbours + k]] for k in range(neighbours)]
@@ -104,11 +115,14 @@
         pieces[s][1] = acc[pl.ds(first, share), :]
 
 
-def start_kernel(x, count, out, col_right, col_left, row_low, row_high):
+def start_kernel(x_hbm, count, out, col_right, col_left, row_low, row_high, x, sems):
     rows, cols, columns, basis = x.shape
+    for r in range(rows):
+        pltpu.make_async_copy(x_hbm.at[r], x.at[r], sems.at[r]).start()
     lane = lax.broadcasted_iota(jnp.int32, (columns, basis), 1)
 
     def one(r, c):
+        pltpu.make_async_copy(x_hbm.at[r], x.at[r], sems.at[r]).wait()
         for j in range(cols):
             value = jnp.where(lane < count[r, j], x[r, j].astype(F32), 0.0).astype(BF16)
             out[r, j] = value
@@ -124,6 +138,17 @@
         row_high[0, j] = out[0, j]
 
 
+def load_kernel(self_hbm, near_hbm, selfs, near, sems):
+    copies = []
+    for r in range(selfs.shape[0]):
+        copies.append(pltpu.make_async_copy(self_hbm.at[r], selfs.at[r], sems.at[0, r]))
+        copies.append(pltpu.make_async_copy(near_hbm.at[r], near.at[r], sems.at[1, r]))
+    for c in copies:
+        c.start()
+    for c in copies:
+        c.wait()
+
+
 def relay_kernel(low, high, send_right, send_left):
     cols = low.shape[1]
     for t, halo in enumerate((low, high)):
@@ -131,16 +156,21 @@
         send_left[t, 0] = halo[0, 0]
 
 
-def gram_kernel(v, gram):
+def gram_kernel(v, gram, whole, sems):
     rows, cols = v.shape[:2]
+    copies = [pltpu.make_async_copy(v.at[r], whole.at[r], sems.at[r]) for r in range(rows)]
+    for c in copies:
+        c.start()
     gram[...] = jnp.zeros_like(gram)
 
-    def one(r, c):
+    def one(r, carry):
         wide_v = jnp.concatenate([v[r, j] for j in range(cols)], axis=1)
         gram[...] += nt_dot(wide_v, wide_v)
-        return c
+        return carry
 
     lax.fori_loop(0, rows, one, 0)
+    for c in copies:
+        c.wait()
 
 
 def shifted(value, axes, count, step):
@@ -170,9 +200,18 @@
     square = jax.ShapeDtypeStruct((columns, columns), F32)
     per_element = 2 * columns * basis * basis * (neighbours + 1)
 
-    current = call(start_kernel, block, [x_block, basis_counts], in_specs=[VMEM, SMEM])
-    older, gram = None, None
-    for mode in ("first", "second", "third", "image"):
+    x_hbm, self_hbm, near_hbm = (
+        pltpu.with_memory_space_constraint(a, pltpu.HBM) for a in (x_block, h_self, h_near)
+    )
+    current = call(
+        start_kernel,
+        block,
+        [x_hbm, basis_counts],
+        in_specs=[HBM, SMEM],
+        scratch=[pltpu.VMEM(x_block.shape, BF16), pltpu.SemaphoreType.DMA((rows,))],
+    )
+    older = None
+    for step, mode in enumerate(("first", "second", "third", "image")):
         v, col_right, col_left, row_low, row_high = current
         left = shifted(col_right, band, n_band, 1)
         right = shifted(col_left, band, n_band, -1)
@@ -182,16 +221,39 @@
         send_right, send_left = call(relay_kernel, relay, [low, high])
         corner_left = shifted(send_right, band, n_band, 1)
         corner_right = shifted(send_left, band, n_band, -1)
+        if step == 0:
+            resident = call(
+                load_kernel,
+                [jax.ShapeDtypeStruct(a.shape, BF16) for a in (h_self, h_near)],
+                [self_hbm, near_hbm],
+                in_specs=[HBM, HBM],
+                scratch=[pltpu.SemaphoreType.DMA((2, rows))],
+            )
         prev = [older] if mode in ("second", "third") else []
         args = [index, basis_counts, v, low, high, left, right, corner_left, corner_right]
-        args += [h_self, h_near, *prev]
-        specs = [SMEM, SMEM] + [VMEM] * (len(args) - 2)
-        scratch = [pltpu.VMEM(((rows + 2) * wide, columns, basis), BF16)]
-        if mode == "image":
-            gram = call(gram_kernel, square, [v], flops=2 * 32 * columns * columns * basis)
+        args += [self_hbm, near_hbm] if mode == "image" else [*resident, *prev]
+        specs = [SMEM, SMEM] + [VMEM] * 7 + [HBM if mode == "image" else VMEM] * 2
+        specs += [VMEM] * len(prev)
+        scratch = [
+            pltpu.VMEM(((rows + 2) * wide, columns, basis), BF16),
+        ]
+        if mode == "image":
+            gram, filtered = call(
+                gram_kernel,
+                [square, block[0]],
+                [v],
+                out_specs=[VMEM, HBM],
+                scratch=[pltpu.SemaphoreType.DMA((rows,))],
+                flops=2 * rows * cols * columns * columns * basis,
+            )
             args += [band_at, gram]
             specs += [SMEM, VMEM]
-            scratch.append(pltpu.VMEM((columns, columns), F32))
+            scratch += [
+                pltpu.VMEM((columns, columns), F32),
+                pltpu.VMEM(h_self.shape, BF16),
+                pltpu.VMEM(h_near.shape, BF16),
+                pltpu.SemaphoreType.DMA((2, rows)),
+            ]
             out_shape = [jax.ShapeDtypeStruct((2, columns // 4, columns), F32)] * 4
         else:
             out_shape = block
@@ -204,9 +266,9 @@
             flops=32 * per_element,
         )
         if mode == "image":
-            filtered, pieces = v, done
+            pieces = done
         else:
-            older, current = v, done
+            older, current = v, done[:5]
 
     total = pieces[0]
     for s in range(1, n_band):
@@ -218,8 +280,9 @@
 
     total = fold(total, "x", [[(p, (p + s) % 4) for p in range(4)] for s in (1, 2, 3)])
     total = fold(total, "yl", [[(p, 1 - p) for p in range(2)]])
-    for pairs in ([(p, p ^ 1) for p in range(8)], [(p, p ^ 2) for p in range(8)], [(p, 7 - p) for p in range(8)]):
-        total = fold(total, "z", [pairs])
+    total = fold(total, "z", [[(p, p ^ 1) for p in range(8)]])
+    total = fold(total, "z", [[(p, p ^ 2) for p in range(8)]])
+    total = fold(total, "z", [[(p, 7 - p) for p in range(8)]])
     normalizer = jnp.float32(rows * cols * n_elem * n_band * basis / 3.0)
     total = total / normalizer
     return filtered, total[0], total[1]

time: 151 us -> 144 us (0.954)
  local copies, waits for them, and re-layouts: 9.88 us -> 1.59 us
  Pallas kernels: 25.3 us -> 28.6 us
  waiting for transfers between devices: 45.8 us -> 43.1 us
    unnamed x17 -> x3, local copies, waits for them, and re-layouts: 9.05 us -> 0.77 us
    pallas_call x10 -> x11, Pallas kernels: 25.3 us -> 28.6 us  [call(): pl.pallas_call(body, out_shape=out_shape, in_specs=in_specs or [VMEM] * l...]
    ppermute x27, waiting for transfers between devices: 24.8 us -> 22.1 us  [shifted(): lax.ppermute(value, axes, [(p, (p + step) % count) for p in range(count)])]
  transfers between devices with their start and end apart: 34 -> 34, of which waited for: 16 -> 18; matrix products, arithmetic and copies ran while one was open for 0% -> 0% of each run, Pallas kernels for 2% -> 4%
where the time goes in v3:
time: 144 us
  starting transfers between devices  69.4 us (48%)
  waiting for transfers between devices  43.1 us (30%)
  Pallas kernels  28.6 us (20%)
  local copies, waits for them, and re-layouts  1.59 us (1%)
    ppermute x27, starting transfers between devices, shifted(): lax.ppermute(value, axes, [(p, (p + step) % count) for p in range(count)])  48.3 us
    pallas_call x11, Pallas kernels, call(): pl.pallas_call(body, out_shape=out_shape, in_specs=in_specs or [VMEM] * l...  28.6 us
    ppermute x27, waiting for transfers between devices, shifted(): lax.ppermute(value, axes, [(p, (p + step) % count) for p in range(count)])  22.1 us
    ppermute x7, starting transfers between devices, fold(): moved = [lax.ppermute(value, axis, pairs) for pairs in maps]  21.1 us
    ppermute x7, waiting for transfers between devices, fold(): moved = [lax.ppermute(value, axis, pairs) for pairs in maps]  20.9 us
  transfers between devices with their start and end apart: 34, of which 18 were waited for; matrix products, arithmetic and copies ran while one was open for 0% of the time, Pallas kernels for 4%

profile of v3, /device:TPU:40, one launch (start us, length us, event | category | flops | bytes accessed | tf_op | source)
XLA Modules:
  0.0 143.6 jit_solution(10807833921497907334)
XLA Ops:
  1.4 2.1 %shard_map.76 = (bf16[8,4,160,128]{3,2,1,0:T(8,128)(2,1)S(1)}, bf16[8,1,160,128]{3,2,1,0:T(8,128)(2,1)S(1)}, bf16[8,1,160,128]{3,2,1,0:T(8,128)(2,1)S(1)}, bf16[...) custom-call(bf16[8,4,160,128]{3,2,1,0:T(8,128)(2,1)} %x_hbm.1, s32[8,4]{1,0:T(8,128)S(1)} %copy.18.count.refs_1_), custom_call_target="tpu_custom_call" | custom-call | bytes 8000000 | tf_op jit(solution)/shard_map/pallas_call | solution.py:24
  5.1 2.6 %collective-permute-start.1 = (bf16[1,4,160,128]{3,2,1,0:T(8,128)(2,1)S(1)}, bf16[1,4,160,128]{3,2,1,0:T(8,128)(2,1)S(1)}, u32[]{:S(2)}, u32[]{:S(2)}) collective-permute-start(bf16[1,4,160,128]{3,2,1,0:T(8,128)(2,1)S(1)} %get-tuple-element.41), channel_id=1, source_target_pairs={{0,252},{4,0},{8,4},{12,8},{16,12},{20,16},{24,20},{28,24},{32,28}... | collective-permute-start | bytes 491528 | tf_op jit(solution)/shard_map/ppermute | solution.py:177
  7.7 3.2 %collective-permute-start.3 = (bf16[8,1,160,128]{3,2,1,0:T(8,128)(2,1)S(1)}, bf16[8,1,160,128]{3,2,1,0:T(8,128)(2,1)S(1)}, u32[]{:S(2)}, u32[]{:S(2)}) collective-permute-start(bf16[8,1,160,128]{3,2,1,0:T(8,128)(2,1)S(1)} %get-tuple-element.43), channel_id=1, source_target_pairs={{0,3},{1,0},{2,1},{3,2},{4,7},{5,4},{6,5},{7,6},{8,11},{9,8},{10,9... | collective-permute-start | bytes 983048 | tf_op jit(solution)/shard_map/ppermute | solution.py:177
  11.8 3.2 %collective-permute-start.5 = (bf16[2,1,160,128]{3,2,1,0:T(8,128)(2,1)S(1)}, bf16[2,1,160,128]{3,2,1,0:T(8,128)(2,1)S(1)}, u32[]{:S(2)}, u32[]{:S(2)}) collective-permute-start(bf16[2,1,160,128]{3,2,1,0:T(8,128)(2,1)S(1)} %get-tuple-element.45), channel_id=1, source_target_pairs={{0,3},{1,0},{2,1},{3,2},{4,7},{5,4},{6,5},{7,6},{8,11},{9,8},{10,9... | collective-permute-start | bytes 245768 | tf_op jit(solution)/shard_map/ppermute | solution.py:177
  15.2 3.3 %shard_map.78 = (bf16[8,4,128,128]{3,2,1,0:T(8,128)(2,1)S(1)}, bf16[8,4,6,128,128]{4,3,2,1,0:T(8,128)(2,1)S(1)}) custom-call(bf16[8,4,128,128]{3,2,1,0:T(8,128)(2,1)} %refs_9_.1, bf16[8,4,6,128,128]{4,3,2,1,0:T(8,128)(2,1)} %refs_10_.1), custom_call_target="tpu_custom_call" | custom-call | bytes 8000000 | tf_op jit(solution)/shard_map/pallas_call | solution.py:24
  18.5 2.6 %collective-permute-done.4.refs_7_ = bf16[2,1,160,128]{3,2,1,0:T(8,128)(2,1)S(1)} collective-permute-done((bf16[2,1,160,128]{3,2,1,0:T(8,128)(2,1)S(1)}, bf16[2,1,160,128]{3,2,1,0:T(8,128)(2,1)S(1)}, u32[]{:S(2)}, u32[]{:S(2)}) %collective-permute-start.4) | collective-permute-done | bytes 81952 | tf_op jit(solution)/shard_map/ppermute | solution.py:177
  21.1 4.6 %shard_map.79 = (bf16[8,4,160,128]{3,2,1,0:T(8,128)(2,1)S(1)}, bf16[8,1,160,128]{3,2,1,0:T(8,128)(2,1)S(1)}, bf16[8,1,160,128]{3,2,1,0:T(8,128)(2,1)S(1)}, bf16[...) custom-call(s32[8,24]{1,0:T(8,128)S(1)} %reshape.12.refs_0_, s32[8,4]{1,0:T(8,128)S(1)} %copy.18.count.refs_1_, ...), custom_call_target="tpu_custom_call" | custom-call | flops 1174405120 | bytes 8000000 | tf_op jit(solution)/shard_map/pallas_call | solution.py:24
  26.9 2.2 %collective-permute-start.9 = (bf16[8,1,160,128]{3,2,1,0:T(8,128)(2,1)S(1)}, bf16[8,1,160,128]{3,2,1,0:T(8,128)(2,1)S(1)}, u32[]{:S(2)}, u32[]{:S(2)}) collective-permute-start(bf16[8,1,160,128]{3,2,1,0:T(8,128)(2,1)S(1)} %get-tuple-element.52), channel_id=1, source_target_pairs={{0,3},{1,0},{2,1},{3,2},{4,7},{5,4},{6,5},{7,6},{8,11},{9,8},{10,9... | collective-permute-start | bytes 983048 | tf_op jit(solution)/shard_map/ppermute | solution.py:177
  29.1 4.1 %collective-permute-start.7 = (bf16[1,4,160,128]{3,2,1,0:T(8,128)(2,1)S(1)}, bf16[1,4,160,128]{3,2,1,0:T(8,128)(2,1)S(1)}, u32[]{:S(2)}, u32[]{:S(2)}) collective-permute-start(bf16[1,4,160,128]{3,2,1,0:T(8,128)(2,1)S(1)} %get-tuple-element.50), channel_id=1, source_target_pairs={{0,252},{4,0},{8,4},{12,8},{16,12},{20,16},{24,20},{28,24},{32,28}... | collective-permute-start | bytes 491528 | tf_op jit(solution)/shard_map/ppermute | solution.py:177
  33.2 4.0 %collective-permute-done.6.low.refs_3_ = bf16[1,4,160,128]{3,2,1,0:T(8,128)(2,1)S(1)} collective-permute-done((bf16[1,4,160,128]{3,2,1,0:T(8,128)(2,1)S(1)}, bf16[1,4,160,128]{3,2,1,0:T(8,128)(2,1)S(1)}, u32[]{:S(2)}, u32[]{:S(2)}) %collective-permute-start.6) | collective-permute-done | bytes 163872 | tf_op jit(solution)/shard_map/ppermute | solution.py:177
  37.3 3.2 %collective-permute-start.11 = (bf16[2,1,160,128]{3,2,1,0:T(8,128)(2,1)S(1)}, bf16[2,1,160,128]{3,2,1,0:T(8,128)(2,1)S(1)}, u32[]{:S(2)}, u32[]{:S(2)}) collective-permute-start(bf16[2,1,160,128]{3,2,1,0:T(8,128)(2,1)S(1)} %get-tuple-element.54), channel_id=1, source_target_pairs={{0,3},{1,0},{2,1},{3,2},{4,7},{5,4},{6,5},{7,6},{8,11},{9,8},{10,9... | collective-permute-start | bytes 245768 | tf_op jit(solution)/shard_map/ppermute | solution.py:177
  40.6 2.1 %collective-permute-done.10.refs_7_ = bf16[2,1,160,128]{3,2,1,0:T(8,128)(2,1)S(1)} collective-permute-done((bf16[2,1,160,128]{3,2,1,0:T(8,128)(2,1)S(1)}, bf16[2,1,160,128]{3,2,1,0:T(8,128)(2,1)S(1)}, u32[]{:S(2)}, u32[]{:S(2)}) %collective-permute-start.10) | collective-permute-done | bytes 81952 | tf_op jit(solution)/shard_map/ppermute | solution.py:177
  42.7 4.7 %shard_map.81 = (bf16[8,4,160,128]{3,2,1,0:T(8,128)(2,1)S(1)}, bf16[8,1,160,128]{3,2,1,0:T(8,128)(2,1)S(1)}, bf16[8,1,160,128]{3,2,1,0:T(8,128)(2,1)S(1)}, bf16[...) custom-call(s32[8,24]{1,0:T(8,128)S(1)} %reshape.12.refs_0_, s32[8,4]{1,0:T(8,128)S(1)} %copy.18.count.refs_1_, ...), custom_call_target="tpu_custom_call" | custom-call | flops 1174405120 | bytes 8000000 | tf_op jit(solution)/shard_map/pallas_call | solution.py:24
  50.8 4.1 %collective-permute-start.13 = (bf16[1,4,160,128]{3,2,1,0:T(8,128)(2,1)S(1)}, bf16[1,4,160,128]{3,2,1,0:T(8,128)(2,1)S(1)}, u32[]{:S(2)}, u32[]{:S(2)}) collective-permute-start(bf16[1,4,160,128]{3,2,1,0:T(8,128)(2,1)S(1)} %get-tuple-element.57), channel_id=1, source_target_pairs={{0,252},{4,0},{8,4},{12,8},{16,12},{20,16},{24,20},{28,24},{32,28}... | collective-permute-start | bytes 491528 | tf_op jit(solution)/shard_map/ppermute | solution.py:177
  54.9 3.8 %collective-permute-done.12.low.refs_3_ = bf16[1,4,160,128]{3,2,1,0:T(8,128)(2,1)S(1)} collective-permute-done((bf16[1,4,160,128]{3,2,1,0:T(8,128)(2,1)S(1)}, bf16[1,4,160,128]{3,2,1,0:T(8,128)(2,1)S(1)}, u32[]{:S(2)}, u32[]{:S(2)}) %collective-permute-start.12) | collective-permute-done | bytes 163872 | tf_op jit(solution)/shard_map/ppermute | solution.py:177
  58.8 3.2 %collective-permute-start.17 = (bf16[2,1,160,128]{3,2,1,0:T(8,128)(2,1)S(1)}, bf16[2,1,160,128]{3,2,1,0:T(8,128)(2,1)S(1)}, u32[]{:S(2)}, u32[]{:S(2)}) collective-permute-start(bf16[2,1,160,128]{3,2,1,0:T(8,128)(2,1)S(1)} %get-tuple-element.61), channel_id=1, source_target_pairs={{0,3},{1,0},{2,1},{3,2},{4,7},{5,4},{6,5},{7,6},{8,11},{9,8},{10,9... | collective-permute-start | bytes 245768 | tf_op jit(solution)/shard_map/ppermute | solution.py:177
  62.1 2.1 %collective-permute-done.16.refs_7_ = bf16[2,1,160,128]{3,2,1,0:T(8,128)(2,1)S(1)} collective-permute-done((bf16[2,1,160,128]{3,2,1,0:T(8,128)(2,1)S(1)}, bf16[2,1,160,128]{3,2,1,0:T(8,128)(2,1)S(1)}, u32[]{:S(2)}, u32[]{:S(2)}) %collective-permute-start.16) | collective-permute-done | bytes 81952 | tf_op jit(solution)/shard_map/ppermute | solution.py:177
  64.2 4.7 %shard_map.83 = (bf16[8,4,160,128]{3,2,1,0:T(8,128)(2,1)S(1)}, bf16[8,1,160,128]{3,2,1,0:T(8,128)(2,1)S(1)}, bf16[8,1,160,128]{3,2,1,0:T(8,128)(2,1)S(1)}, bf16[...) custom-call(s32[8,24]{1,0:T(8,128)S(1)} %reshape.12.refs_0_, s32[8,4]{1,0:T(8,128)S(1)} %copy.18.count.refs_1_, ...), custom_call_target="tpu_custom_call" | custom-call | flops 1174405120 | bytes 8000000 | tf_op jit(solution)/shard_map/pallas_call | solution.py:24
  72.3 2.3 %collective-permute-start.18 = (bf16[1,4,160,128]{3,2,1,0:T(8,128)(2,1)S(1)}, bf16[1,4,160,128]{3,2,1,0:T(8,128)(2,1)S(1)}, u32[]{:S(2)}, u32[]{:S(2)}) collective-permute-start(bf16[1,4,160,128]{3,2,1,0:T(8,128)(2,1)S(1)} %get-tuple-element.64), channel_id=1, source_target_pairs={{0,4},{4,8},{8,12},{12,16},{16,20},{20,24},{24,28},{28,32},{32,36}... | collective-permute-start | bytes 491528 | tf_op jit(solution)/shard_map/ppermute | solution.py:177
  76.5 3.3 %collective-permute-done.18.low.refs_3_ = bf16[1,4,160,128]{3,2,1,0:T(8,128)(2,1)S(1)} collective-permute-done((bf16[1,4,160,128]{3,2,1,0:T(8,128)(2,1)S(1)}, bf16[1,4,160,128]{3,2,1,0:T(8,128)(2,1)S(1)}, u32[]{:S(2)}, u32[]{:S(2)}) %collective-permute-start.18) | collective-permute-done | bytes 163872 | tf_op jit(solution)/shard_map/ppermute | solution.py:177
  80.0 3.2 %collective-permute-start.23 = (bf16[2,1,160,128]{3,2,1,0:T(8,128)(2,1)S(1)}, bf16[2,1,160,128]{3,2,1,0:T(8,128)(2,1)S(1)}, u32[]{:S(2)}, u32[]{:S(2)}) collective-permute-start(bf16[2,1,160,128]{3,2,1,0:T(8,128)(2,1)S(1)} %get-tuple-element.69), channel_id=1, source_target_pairs={{0,3},{1,0},{2,1},{3,2},{4,7},{5,4},{6,5},{7,6},{8,11},{9,8},{10,9... | collective-permute-start | bytes 245768 | tf_op jit(solution)/shard_map/ppermute | solution.py:177
  85.4 7.4 %shard_map.86 = (f32[2,40,160]{2,1,0:T(8,128)S(1)}, f32[2,40,160]{2,1,0:T(8,128)S(1)}, f32[2,40,160]{2,1,0:T(8,128)S(1)}, f32[2,40,160]{2,1,0:T(8,128)S(1)}) custom-call(s32[8,24]{1,0:T(8,128)S(1)} %reshape.12.refs_0_, s32[8,4]{1,0:T(8,128)S(1)} %copy.18.count.refs_1_, bf16[8,4,160,128]{3,2,1,0:T(8,128)(2,1)S(1)} %get-tuple-element.62.v.refs_2_, ...), custom_call_target="tpu_custom_call" | custom-call | flops 1174405120 | bytes 8000000 | tf_op jit(solution)/shard_map/pallas_call | solution.py:24
  98.2 2.6 %collective-permute-done.25 = f32[2,40,160]{2,1,0:T(8,128)S(1)} collective-permute-done((f32[2,40,160]{2,1,0:T(8,128)S(1)}, f32[2,40,160]{2,1,0:T(8,128)S(1)}, u32[]{:S(2)}, u32[]{:S(2)}) %collective-permute-start.25) | collective-permute-done | bytes 51232 | tf_op jit(solution)/shard_map/ppermute | solution.py:177
  100.8 3.3 %collective-permute-start.27 = (f32[2,40,160]{2,1,0:T(8,128)S(1)}, f32[2,40,160]{2,1,0:T(8,128)S(1)}, u32[]{:S(2)}, u32[]{:S(2)}) collective-permute-start(f32[2,40,160]{2,1,0:T(8,128)S(1)} %add_add_fusion.1), channel_id=1, source_target_pairs={{0,4},{4,8},{8,12},{12,0},{1,5},{5,9},{9,13},{13,1},{2,6},{6,10},{... | collective-permute-start | bytes 153608 | tf_op jit(solution)/shard_map/ppermute | solution.py:278
  104.1 5.1 %collective-permute-start.28 = (f32[2,40,160]{2,1,0:T(8,128)S(1)}, f32[2,40,160]{2,1,0:T(8,128)S(1)}, u32[]{:S(2)}, u32[]{:S(2)}) collective-permute-start(f32[2,40,160]{2,1,0:T(8,128)S(1)} %add_add_fusion.1), channel_id=1, source_target_pairs={{0,8},{4,12},{8,0},{12,4},{1,9},{5,13},{9,1},{13,5},{2,10},{6,14},... | collective-permute-start | bytes 153608 | tf_op jit(solution)/shard_map/ppermute | solution.py:278
  110.3 3.5 %collective-permute-done.28 = f32[2,40,160]{2,1,0:T(8,128)S(1)} collective-permute-done((f32[2,40,160]{2,1,0:T(8,128)S(1)}, f32[2,40,160]{2,1,0:T(8,128)S(1)}, u32[]{:S(2)}, u32[]{:S(2)}) %collective-permute-start.28) | collective-permute-done | bytes 51232 | tf_op jit(solution)/shard_map/ppermute | solution.py:278
  114.6 4.4 %collective-permute-done.30 = f32[2,40,160]{2,1,0:T(8,128)S(1)} collective-permute-done((f32[2,40,160]{2,1,0:T(8,128)S(1)}, f32[2,40,160]{2,1,0:T(8,128)S(1)}, u32[]{:S(2)}, u32[]{:S(2)}) %collective-permute-start.30) | collective-permute-done | bytes 51232 | tf_op jit(solution)/shard_map/ppermute | solution.py:278
  119.0 4.0 %collective-permute-start.31 = (f32[2,40,160]{2,1,0:T(8,128)S(1)}, f32[2,40,160]{2,1,0:T(8,128)S(1)}, u32[]{:S(2)}, u32[]{:S(2)}) collective-permute-start(f32[2,40,160]{2,1,0:T(8,128)S(1)} %add.60), channel_id=1, source_target_pairs={{0,32},{32,0},{64,96},{96,64},{128,160},{160,128},{192,224},{224,1... | collective-permute-start | bytes 153608 | tf_op jit(solution)/shard_map/ppermute | solution.py:278
  123.0 2.4 %collective-permute-done.31 = f32[2,40,160]{2,1,0:T(8,128)S(1)} collective-permute-done((f32[2,40,160]{2,1,0:T(8,128)S(1)}, f32[2,40,160]{2,1,0:T(8,128)S(1)}, u32[]{:S(2)}, u32[]{:S(2)}) %collective-permute-start.31) | collective-permute-done | bytes 51232 | tf_op jit(solution)/shard_map/ppermute | solution.py:278
  125.5 7.5 %collective-permute-start.32 = (f32[2,40,160]{2,1,0:T(8,128)S(1)}, f32[2,40,160]{2,1,0:T(8,128)S(1)}, u32[]{:S(2)}, u32[]{:S(2)}) collective-permute-start(f32[2,40,160]{2,1,0:T(8,128)S(1)} %add.61), channel_id=1, source_target_pairs={{0,64},{32,96},{64,0},{96,32},{128,192},{160,224},{192,128},{224,1... | collective-permute-start | bytes 153608 | tf_op jit(solution)/shard_map/ppermute | solution.py:278
  133.0 2.4 %collective-permute-done.32 = f32[2,40,160]{2,1,0:T(8,128)S(1)} collective-permute-done((f32[2,40,160]{2,1,0:T(8,128)S(1)}, f32[2,40,160]{2,1,0:T(8,128)S(1)}, u32[]{:S(2)}, u32[]{:S(2)}) %collective-permute-start.32) | collective-permute-done | bytes 51232 | tf_op jit(solution)/shard_map/ppermute | solution.py:278
  136.5 6.5 %collective-permute-done.33 = f32[2,40,160]{2,1,0:T(8,128)S(1)} collective-permute-done((f32[2,40,160]{2,1,0:T(8,128)S(1)}, f32[2,40,160]{2,1,0:T(8,128)S(1)}, u32[]{:S(2)}, u32[]{:S(2)}) %collective-permute-start.33) | collective-permute-done | bytes 51232 | tf_op jit(solution)/shard_map/ppermute | solution.py:278
  (60 shorter events, 24.8 us)
Async XLA Ops:
  3.5 8.1 %collective-permute-start = (bf16[1,4,160,128]{3,2,1,0:T(8,128)(2,1)S(1)}, bf16[1,4,160,128]{3,2,1,0:T(8,128)(2,1)S(1)}, u32[]{:S(2)}, u32[]{:S(2)}) collective-permute-start(bf16[1,4,160,128]{3,2,1,0:T(8,128)(2,1)S(1)} %get-tuple-element.40), channel_id=1, source_target_pairs={{0,4},{4,8},{8,12},{12,16},{16,20},{20,24},{24,28},{28,32},{32,36}... | collective-permute-start | bytes 491528 | tf_op jit(solution)/shard_map/ppermute | solution.py:177
  5.1 6.6 %collective-permute-start.1 = (bf16[1,4,160,128]{3,2,1,0:T(8,128)(2,1)S(1)}, bf16[1,4,160,128]{3,2,1,0:T(8,128)(2,1)S(1)}, u32[]{:S(2)}, u32[]{:S(2)}) collective-permute-start(bf16[1,4,160,128]{3,2,1,0:T(8,128)(2,1)S(1)} %get-tuple-element.41), channel_id=1, source_target_pairs={{0,252},{4,0},{8,4},{12,8},{16,12},{20,16},{24,20},{28,24},{32,28}... | collective-permute-start | bytes 491528 | tf_op jit(solution)/shard_map/ppermute | solution.py:177
  7.7 13.3 %collective-permute-start.2 = (bf16[8,1,160,128]{3,2,1,0:T(8,128)(2,1)S(1)}, bf16[8,1,160,128]{3,2,1,0:T(8,128)(2,1)S(1)}, u32[]{:S(2)}, u32[]{:S(2)}) collective-permute-start(bf16[8,1,160,128]{3,2,1,0:T(8,128)(2,1)S(1)} %get-tuple-element.42), channel_id=1, source_target_pairs={{0,1},{1,2},{2,3},{3,0},{4,5},{5,6},{6,7},{7,4},{8,9},{9,10},{10,1... | collective-permute-start | bytes 983048 | tf_op jit(solution)/shard_map/ppermute | solution.py:177
  7.7 13.3 %collective-permute-start.3 = (bf16[8,1,160,128]{3,2,1,0:T(8,128)(2,1)S(1)}, bf16[8,1,160,128]{3,2,1,0:T(8,128)(2,1)S(1)}, u32[]{:S(2)}, u32[]{:S(2)}) collective-permute-start(bf16[8,1,160,128]{3,2,1,0:T(8,128)(2,1)S(1)} %get-tuple-element.43), channel_id=1, source_target_pairs={{0,3},{1,0},{2,1},{3,2},{4,7},{5,4},{6,5},{7,6},{8,11},{9,8},{10,9... | collective-permute-start | bytes 983048 | tf_op jit(solution)/shard_map/ppermute | solution.py:177
  11.7 9.4 %collective-permute-start.4 = (bf16[2,1,160,128]{3,2,1,0:T(8,128)(2,1)S(1)}, bf16[2,1,160,128]{3,2,1,0:T(8,128)(2,1)S(1)}, u32[]{:S(2)}, u32[]{:S(2)}) collective-permute-start(bf16[2,1,160,128]{3,2,1,0:T(8,128)(2,1)S(1)} %get-tuple-element.44), channel_id=1, source_target_pairs={{0,1},{1,2},{2,3},{3,0},{4,5},{5,6},{6,7},{7,4},{8,9},{9,10},{10,1... | collective-permute-start | bytes 245768 | tf_op jit(solution)/shard_map/ppermute | solution.py:177
  11.8 9.3 %collective-permute-start.5 = (bf16[2,1,160,128]{3,2,1,0:T(8,128)(2,1)S(1)}, bf16[2,1,160,128]{3,2,1,0:T(8,128)(2,1)S(1)}, u32[]{:S(2)}, u32[]{:S(2)}) collective-permute-start(bf16[2,1,160,128]{3,2,1,0:T(8,128)(2,1)S(1)} %get-tuple-element.45), channel_id=1, source_target_pairs={{0,3},{1,0},{2,1},{3,2},{4,7},{5,4},{6,5},{7,6},{8,11},{9,8},{10,9... | collective-permute-start | bytes 245768 | tf_op jit(solution)/shard_map/ppermute | solution.py:177
  25.7 17.0 %collective-permute-start.8 = (bf16[8,1,160,128]{3,2,1,0:T(8,128)(2,1)S(1)}, bf16[8,1,160,128]{3,2,1,0:T(8,128)(2,1)S(1)}, u32[]{:S(2)}, u32[]{:S(2)}) collective-permute-start(bf16[8,1,160,128]{3,2,1,0:T(8,128)(2,1)S(1)} %get-tuple-element.51), channel_id=1, source_target_pairs={{0,1},{1,2},{2,3},{3,0},{4,5},{5,6},{6,7},{7,4},{8,9},{9,10},{10,1... | collective-permute-start | bytes 983048 | tf_op jit(solution)/shard_map/ppermute | solution.py:177
  26.9 15.8 %collective-permute-start.9 = (bf16[8,1,160,128]{3,2,1,0:T(8,128)(2,1)S(1)}, bf16[8,1,160,128]{3,2,1,0:T(8,128)(2,1)S(1)}, u32[]{:S(2)}, u32[]{:S(2)}) collective-permute-start(bf16[8,1,160,128]{3,2,1,0:T(8,128)(2,1)S(1)} %get-tuple-element.52), channel_id=1, source_target_pairs={{0,3},{1,0},{2,1},{3,2},{4,7},{5,4},{6,5},{7,6},{8,11},{9,8},{10,9... | collective-permute-start | bytes 983048 | tf_op jit(solution)/shard_map/ppermute | solution.py:177
  29.1 8.2 %collective-permute-start.6 = (bf16[1,4,160,128]{3,2,1,0:T(8,128)(2,1)S(1)}, bf16[1,4,160,128]{3,2,1,0:T(8,128)(2,1)S(1)}, u32[]{:S(2)}, u32[]{:S(2)}) collective-permute-start(bf16[1,4,160,128]{3,2,1,0:T(8,128)(2,1)S(1)} %get-tuple-element.49), channel_id=1, source_target_pairs={{0,4},{4,8},{8,12},{12,16},{16,20},{20,24},{24,28},{28,32},{32,36}... | collective-permute-start | bytes 491528 | tf_op jit(solution)/shard_map/ppermute | solution.py:177
  29.1 8.2 %collective-permute-start.7 = (bf16[1,4,160,128]{3,2,1,0:T(8,128)(2,1)S(1)}, bf16[1,4,160,128]{3,2,1,0:T(8,128)(2,1)S(1)}, u32[]{:S(2)}, u32[]{:S(2)}) collective-permute-start(bf16[1,4,160,128]{3,2,1,0:T(8,128)(2,1)S(1)} %get-tuple-element.50), channel_id=1, source_target_pairs={{0,252},{4,0},{8,4},{12,8},{16,12},{20,16},{24,20},{28,24},{32,28}... | collective-permute-start | bytes 491528 | tf_op jit(solution)/shard_map/ppermute | solution.py:177
  37.2 5.4 %collective-permute-start.10 = (bf16[2,1,160,128]{3,2,1,0:T(8,128)(2,1)S(1)}, bf16[2,1,160,128]{3,2,1,0:T(8,128)(2,1)S(1)}, u32[]{:S(2)}, u32[]{:S(2)}) collective-permute-start(bf16[2,1,160,128]{3,2,1,0:T(8,128)(2,1)S(1)} %get-tuple-element.53), channel_id=1, source_target_pairs={{0,1},{1,2},{2,3},{3,0},{4,5},{5,6},{6,7},{7,4},{8,9},{9,10},{10,1... | collective-permute-start | bytes 245768 | tf_op jit(solution)/shard_map/ppermute | solution.py:177
  37.3 5.4 %collective-permute-start.11 = (bf16[2,1,160,128]{3,2,1,0:T(8,128)(2,1)S(1)}, bf16[2,1,160,128]{3,2,1,0:T(8,128)(2,1)S(1)}, u32[]{:S(2)}, u32[]{:S(2)}) collective-permute-start(bf16[2,1,160,128]{3,2,1,0:T(8,128)(2,1)S(1)} %get-tuple-element.54), channel_id=1, source_target_pairs={{0,3},{1,0},{2,1},{3,2},{4,7},{5,4},{6,5},{7,6},{8,11},{9,8},{10,9... | collective-permute-start | bytes 245768 | tf_op jit(solution)/shard_map/ppermute | solution.py:177
  47.4 16.8 %collective-permute-start.14 = (bf16[8,1,160,128]{3,2,1,0:T(8,128)(2,1)S(1)}, bf16[8,1,160,128]{3,2,1,0:T(8,128)(2,1)S(1)}, u32[]{:S(2)}, u32[]{:S(2)}) collective-permute-start(bf16[8,1,160,128]{3,2,1,0:T(8,128)(2,1)S(1)} %get-tuple-element.58), channel_id=1, source_target_pairs={{0,1},{1,2},{2,3},{3,0},{4,5},{5,6},{6,7},{7,4},{8,9},{9,10},{10,1... | collective-permute-start | bytes 983048 | tf_op jit(solution)/shard_map/ppermute | solution.py:177
  49.0 15.2 %collective-permute-start.15 = (bf16[8,1,160,128]{3,2,1,0:T(8,128)(2,1)S(1)}, bf16[8,1,160,128]{3,2,1,0:T(8,128)(2,1)S(1)}, u32[]{:S(2)}, u32[]{:S(2)}) collective-permute-start(bf16[8,1,160,128]{3,2,1,0:T(8,128)(2,1)S(1)} %get-tuple-element.59), channel_id=1, source_target_pairs={{0,3},{1,0},{2,1},{3,2},{4,7},{5,4},{6,5},{7,6},{8,11},{9,8},{10,9... | collective-permute-start | bytes 983048 | tf_op jit(solution)/shard_map/ppermute | solution.py:177
  50.8 8.0 %collective-permute-start.12 = (bf16[1,4,160,128]{3,2,1,0:T(8,128)(2,1)S(1)}, bf16[1,4,160,128]{3,2,1,0:T(8,128)(2,1)S(1)}, u32[]{:S(2)}, u32[]{:S(2)}) collective-permute-start(bf16[1,4,160,128]{3,2,1,0:T(8,128)(2,1)S(1)} %get-tuple-element.56), channel_id=1, source_target_pairs={{0,4},{4,8},{8,12},{12,16},{16,20},{20,24},{24,28},{28,32},{32,36}... | collective-permute-start | bytes 491528 | tf_op jit(solution)/shard_map/ppermute | solution.py:177
  50.8 8.0 %collective-permute-start.13 = (bf16[1,4,160,128]{3,2,1,0:T(8,128)(2,1)S(1)}, bf16[1,4,160,128]{3,2,1,0:T(8,128)(2,1)S(1)}, u32[]{:S(2)}, u32[]{:S(2)}) collective-permute-start(bf16[1,4,160,128]{3,2,1,0:T(8,128)(2,1)S(1)} %get-tuple-element.57), channel_id=1, source_target_pairs={{0,252},{4,0},{8,4},{12,8},{16,12},{20,16},{24,20},{28,24},{32,28}... | collective-permute-start | bytes 491528 | tf_op jit(solution)/shard_map/ppermute | solution.py:177
  58.7 5.4 %collective-permute-start.16 = (bf16[2,1,160,128]{3,2,1,0:T(8,128)(2,1)S(1)}, bf16[2,1,160,128]{3,2,1,0:T(8,128)(2,1)S(1)}, u32[]{:S(2)}, u32[]{:S(2)}) collective-permute-start(bf16[2,1,160,128]{3,2,1,0:T(8,128)(2,1)S(1)} %get-tuple-element.60), channel_id=1, source_target_pairs={{0,1},{1,2},{2,3},{3,0},{4,5},{5,6},{6,7},{7,4},{8,9},{9,10},{10,1... | collective-permute-start | bytes 245768 | tf_op jit(solution)/shard_map/ppermute | solution.py:177
  58.8 5.4 %collective-permute-start.17 = (bf16[2,1,160,128]{3,2,1,0:T(8,128)(2,1)S(1)}, bf16[2,1,160,128]{3,2,1,0:T(8,128)(2,1)S(1)}, u32[]{:S(2)}, u32[]{:S(2)}) collective-permute-start(bf16[2,1,160,128]{3,2,1,0:T(8,128)(2,1)S(1)} %get-tuple-element.61), channel_id=1, source_target_pairs={{0,3},{1,0},{2,1},{3,2},{4,7},{5,4},{6,5},{7,6},{8,11},{9,8},{10,9... | collective-permute-start | bytes 245768 | tf_op jit(solution)/shard_map/ppermute | solution.py:177
  68.9 16.5 %collective-permute-start.20 = (bf16[8,1,160,128]{3,2,1,0:T(8,128)(2,1)S(1)}, bf16[8,1,160,128]{3,2,1,0:T(8,128)(2,1)S(1)}, u32[]{:S(2)}, u32[]{:S(2)}) collective-permute-start(bf16[8,1,160,128]{3,2,1,0:T(8,128)(2,1)S(1)} %get-tuple-element.66), channel_id=1, source_target_pairs={{0,1},{1,2},{2,3},{3,0},{4,5},{5,6},{6,7},{7,4},{8,9},{9,10},{10,1... | collective-permute-start | bytes 983048 | tf_op jit(solution)/shard_map/ppermute | solution.py:177
  70.3 15.1 %collective-permute-start.21 = (bf16[8,1,160,128]{3,2,1,0:T(8,128)(2,1)S(1)}, bf16[8,1,160,128]{3,2,1,0:T(8,128)(2,1)S(1)}, u32[]{:S(2)}, u32[]{:S(2)}) collective-permute-start(bf16[8,1,160,128]{3,2,1,0:T(8,128)(2,1)S(1)} %get-tuple-element.67), channel_id=1, source_target_pairs={{0,3},{1,0},{2,1},{3,2},{4,7},{5,4},{6,5},{7,6},{8,11},{9,8},{10,9... | collective-permute-start | bytes 983048 | tf_op jit(solution)/shard_map/ppermute | solution.py:177
  72.3 7.4 %collective-permute-start.18 = (bf16[1,4,160,128]{3,2,1,0:T(8,128)(2,1)S(1)}, bf16[1,4,160,128]{3,2,1,0:T(8,128)(2,1)S(1)}, u32[]{:S(2)}, u32[]{:S(2)}) collective-permute-start(bf16[1,4,160,128]{3,2,1,0:T(8,128)(2,1)S(1)} %get-tuple-element.64), channel_id=1, source_target_pairs={{0,4},{4,8},{8,12},{12,16},{16,20},{20,24},{24,28},{28,32},{32,36}... | collective-permute-start | bytes 491528 | tf_op jit(solution)/shard_map/ppermute | solution.py:177
  74.6 5.3 %collective-permute-start.19 = (bf16[1,4,160,128]{3,2,1,0:T(8,128)(2,1)S(1)}, bf16[1,4,160,128]{3,2,1,0:T(8,128)(2,1)S(1)}, u32[]{:S(2)}, u32[]{:S(2)}) collective-permute-start(bf16[1,4,160,128]{3,2,1,0:T(8,128)(2,1)S(1)} %get-tuple-element.65), channel_id=1, source_target_pairs={{0,252},{4,0},{8,4},{12,8},{16,12},{20,16},{24,20},{28,24},{32,28}... | collective-permute-start | bytes 491528 | tf_op jit(solution)/shard_map/ppermute | solution.py:177
  79.9 5.4 %collective-permute-start.22 = (bf16[2,1,160,128]{3,2,1,0:T(8,128)(2,1)S(1)}, bf16[2,1,160,128]{3,2,1,0:T(8,128)(2,1)S(1)}, u32[]{:S(2)}, u32[]{:S(2)}) collective-permute-start(bf16[2,1,160,128]{3,2,1,0:T(8,128)(2,1)S(1)} %get-tuple-element.68), channel_id=1, source_target_pairs={{0,1},{1,2},{2,3},{3,0},{4,5},{5,6},{6,7},{7,4},{8,9},{9,10},{10,1... | collective-permute-start | bytes 245768 | tf_op jit(solution)/shard_map/ppermute | solution.py:177
  80.0 5.4 %collective-permute-start.23 = (bf16[2,1,160,128]{3,2,1,0:T(8,128)(2,1)S(1)}, bf16[2,1,160,128]{3,2,1,0:T(8,128)(2,1)S(1)}, u32[]{:S(2)}, u32[]{:S(2)}) collective-permute-start(bf16[2,1,160,128]{3,2,1,0:T(8,128)(2,1)S(1)} %get-tuple-element.69), channel_id=1, source_target_pairs={{0,3},{1,0},{2,1},{3,2},{4,7},{5,4},{6,5},{7,6},{8,11},{9,8},{10,9... | collective-permute-start | bytes 245768 | tf_op jit(solution)/shard_map/ppermute | solution.py:177
  92.7 5.4 %collective-permute-start.24 = (f32[2,40,160]{2,1,0:T(8,128)S(1)}, f32[2,40,160]{2,1,0:T(8,128)S(1)}, u32[]{:S(2)}, u32[]{:S(2)}) collective-permute-start(f32[2,40,160]{2,1,0:T(8,128)S(1)} %get-tuple-element.72), channel_id=1, source_target_pairs={{0,1},{1,2},{2,3},{3,0},{4,5},{5,6},{6,7},{7,4},{8,9},{9,10},{10,1... | collective-permute-start | bytes 153608 | tf_op jit(solution)/shard_map/ppermute | solution.py:177
  94.8 6.0 %collective-permute-start.25 = (f32[2,40,160]{2,1,0:T(8,128)S(1)}, f32[2,40,160]{2,1,0:T(8,128)S(1)}, u32[]{:S(2)}, u32[]{:S(2)}) collective-permute-start(f32[2,40,160]{2,1,0:T(8,128)S(1)} %get-tuple-element.73), channel_id=1, source_target_pairs={{0,2},{1,3},{2,0},{3,1},{4,6},{5,7},{6,4},{7,5},{8,10},{9,11},{10,... | collective-permute-start | bytes 153608 | tf_op jit(solution)/shard_map/ppermute | solution.py:177
  100.8 9.5 %collective-permute-start.27 = (f32[2,40,160]{2,1,0:T(8,128)S(1)}, f32[2,40,160]{2,1,0:T(8,128)S(1)}, u32[]{:S(2)}, u32[]{:S(2)}) collective-permute-start(f32[2,40,160]{2,1,0:T(8,128)S(1)} %add_add_fusion.1), channel_id=1, source_target_pairs={{0,4},{4,8},{8,12},{12,0},{1,5},{5,9},{9,13},{13,1},{2,6},{6,10},{... | collective-permute-start | bytes 153608 | tf_op jit(solution)/shard_map/ppermute | solution.py:278
  104.1 9.7 %collective-permute-start.28 = (f32[2,40,160]{2,1,0:T(8,128)S(1)}, f32[2,40,160]{2,1,0:T(8,128)S(1)}, u32[]{:S(2)}, u32[]{:S(2)}) collective-permute-start(f32[2,40,160]{2,1,0:T(8,128)S(1)} %add_add_fusion.1), channel_id=1, source_target_pairs={{0,8},{4,12},{8,0},{12,4},{1,9},{5,13},{9,1},{13,5},{2,10},{6,14},... | collective-permute-start | bytes 153608 | tf_op jit(solution)/shard_map/ppermute | solution.py:278
  109.2 5.2 %collective-permute-start.29 = (f32[2,40,160]{2,1,0:T(8,128)S(1)}, f32[2,40,160]{2,1,0:T(8,128)S(1)}, u32[]{:S(2)}, u32[]{:S(2)}) collective-permute-start(f32[2,40,160]{2,1,0:T(8,128)S(1)} %add_add_fusion.1), channel_id=1, source_target_pairs={{0,12},{4,0},{8,4},{12,8},{1,13},{5,1},{9,5},{13,9},{2,14},{6,2},{... | collective-permute-start | bytes 153608 | tf_op jit(solution)/shard_map/ppermute | solution.py:278
  119.0 6.5 %collective-permute-start.31 = (f32[2,40,160]{2,1,0:T(8,128)S(1)}, f32[2,40,160]{2,1,0:T(8,128)S(1)}, u32[]{:S(2)}, u32[]{:S(2)}) collective-permute-start(f32[2,40,160]{2,1,0:T(8,128)S(1)} %add.60), channel_id=1, source_target_pairs={{0,32},{32,0},{64,96},{96,64},{128,160},{160,128},{192,224},{224,1... | collective-permute-start | bytes 153608 | tf_op jit(solution)/shard_map/ppermute | solution.py:278
  125.5 9.9 %collective-permute-start.32 = (f32[2,40,160]{2,1,0:T(8,128)S(1)}, f32[2,40,160]{2,1,0:T(8,128)S(1)}, u32[]{:S(2)}, u32[]{:S(2)}) collective-permute-start(f32[2,40,160]{2,1,0:T(8,128)S(1)} %add.61), channel_id=1, source_target_pairs={{0,64},{32,96},{64,0},{96,32},{128,192},{160,224},{192,128},{224,1... | collective-permute-start | bytes 153608 | tf_op jit(solution)/shard_map/ppermute | solution.py:278
  135.4 7.5 %collective-permute-start.33 = (f32[2,40,160]{2,1,0:T(8,128)S(1)}, f32[2,40,160]{2,1,0:T(8,128)S(1)}, u32[]{:S(2)}, u32[]{:S(2)}) collective-permute-start(f32[2,40,160]{2,1,0:T(8,128)S(1)} %add.62), channel_id=1, source_target_pairs={{0,224},{32,192},{64,160},{96,128},{128,96},{160,64},{192,32},{224... | collective-permute-start | bytes 153608 | tf_op jit(solution)/shard_map/ppermute | solution.py:278
  (3 other events, 23.2 us)
